TPU v7x, 256 devices: a whole 4x4x8 slice. The times are simulated.
256 devices in a mesh: dp: 8 (over z), ctx: 32 (over x, y, core).
Axes of the slice: x: 4, y: 4, z: 8, core: 2. Of those that a mesh axis runs over, the one named last changes fastest.
Arguments:
- queries: bfloat16 [8, 4096, 4096], P('dp', 'ctx')
- keys: bfloat16 [8, 4096, 4096], P('dp', 'ctx')
- values: bfloat16 [8, 4096, 4096], P('dp', 'ctx'), may hold values from -6 to 6
- d_out: bfloat16 [8, 4096, 4096], P('dp', 'ctx'), may hold values from -6 to 6
- gains: float32 [2, 4096], P(None, 'dp'), may hold values from 0.5 to 2
- window_widths: int32 [32], P('ctx'), may hold values from 0 to 1
- global_blocks: int32 [8, 2], P('dp'), may hold values from 0 to 31, as said below
- random_blocks: int32 [8, 32, 3], P('dp'), may hold values from 0 to 31
Outputs:
- out: bfloat16 [8, 4096, 4096], P('dp', 'ctx')
- d_queries: bfloat16 [8, 4096, 4096], P('dp', 'ctx')
- d_keys: bfloat16 [8, 4096, 4096], P('dp', 'ctx')
- d_values: bfloat16 [8, 4096, 4096], P('dp', 'ctx')
- d_gains: float32 [2, 4096], P(None, 'dp')
Inputs may be any that keep to these rules, and one draw needn't show every extreme that they name: `global_blocks`: the 2 ids of a sequence are different.
All inputs are finite; a program needn't handle non-finite values.
Results may differ from a plain program's by a relative error of at most 0.018.
The roundings to bfloat16 on the way count: a program that leaves them out, or rounds other values in their place, can miss the bound.
Values may be sent and summed in bfloat16 or wider, within the bound.
No kernel may reach another device: no remote copies, remote signals or barrier semaphores. Data moves between devices by JAX's collectives and lax.ppermute only.
A program may use at most 128 MiB of HBM per device.

v0:
```python
import math

import jax
import jax.numpy as jnp
from jax import lax
from jax.sharding import PartitionSpec as P

HD = 128
WMAX = 1


NEG_FILL = -1e30


def slot_table(global_ids, random_ids, widths):
    block_count = random_ids.shape[0]
    blocks = jnp.arange(block_count, dtype=jnp.int32)
    offsets = jnp.arange(-WMAX, WMAX + 1, dtype=jnp.int32)
    nearby = blocks[:, None] + offsets[None, :]
    inside = (nearby >= 0) & (nearby < block_count)
    in_window = jnp.abs(offsets)[None, :] <= widths[:, None]
    window_ok = inside[None, :, :] & in_window[:, None, :]
    global_cols = jnp.broadcast_to(global_ids[None, :], (block_count, global_ids.shape[0]))
    slot_ids = jnp.concatenate([nearby, global_cols, random_ids], axis=1)
    always_on = jnp.ones(
        (widths.shape[0], block_count, global_ids.shape[0] + random_ids.shape[1]), dtype=jnp.bool_
    )
    listed = jnp.concatenate([window_ok, always_on], axis=2)
    slot_total = slot_ids.shape[1]
    matches = slot_ids[:, :, None] == slot_ids[:, None, :]
    position = jnp.arange(slot_total)
    earlier = position[None, :] < position[:, None]
    repeated = jnp.any(matches[None] & earlier[None, None] & listed[:, :, None, :], axis=3)
    usable = listed & jnp.logical_not(repeated)
    return (jnp.clip(slot_ids, 0, block_count - 1), usable)


def softmax_rows(scores):
    row_max = jnp.max(scores, axis=-1, keepdims=True)
    exponent = jnp.exp(scores - row_max)
    return exponent / jnp.sum(exponent, axis=-1, keepdims=True)


def slot_weights(q_group, k_slots, usable_group, block_len, score_scale):
    scores = (
        jnp.einsum("irhd,ijhd->ihrj", q_group, k_slots, preferred_element_type=jnp.float32)
        * score_scale
    )
    allowed = jnp.repeat(usable_group, block_len, axis=2)
    return softmax_rows(jnp.where(allowed[:, :, None, :], scores, NEG_FILL))


def gather_slots(blocks_in, id_group):
    group_len, slot_total = id_group.shape
    picked = blocks_in[id_group]
    return picked.reshape(group_len, slot_total * picked.shape[2], picked.shape[3], picked.shape[4])


def group_layout(block_count, block_len):
    group_len = math.gcd(block_count, max(1, 512 // block_len))
    return (group_len, block_count // group_len)


def forward_pass(q_blocks, k_blocks, v_blocks, slot_ids, usable_t, global_ids, score_scale):
    block_count, block_len, head_count, head_dim = q_blocks.shape
    group_len, step_count = group_layout(block_count, block_len)

    def forward_one_group(running, inputs_now):
        q_group, id_group, usable_group = inputs_now
        k_slots = gather_slots(k_blocks, id_group)
        v_slots = gather_slots(v_blocks, id_group)
        weights_b = slot_weights(q_group, k_slots, usable_group, block_len, score_scale).astype(
            jnp.bfloat16
        )
        attended = jnp.einsum(
            "ihrj,ijhd->irhd", weights_b, v_slots, preferred_element_type=jnp.float32
        )
        return (running, attended.astype(jnp.bfloat16))

    split_inputs = (
        q_blocks.reshape(step_count, group_len, block_len, head_count, head_dim),
        slot_ids.reshape(step_count, group_len, -1),
        usable_t.reshape(step_count, group_len, head_count, -1),
    )
    _, attended = lax.scan(forward_one_group, jnp.zeros((), jnp.int32), split_inputs)
    attended = attended.reshape(block_count, block_len, head_count, head_dim)
    k_flat = k_blocks.reshape(block_count * block_len, head_count, head_dim)
    v_flat = v_blocks.reshape(block_count * block_len, head_count, head_dim)
    full_w = softmax_rows(
        jnp.einsum(
            "grhd,thd->ghrt", q_blocks[global_ids], k_flat, preferred_element_type=jnp.float32
        )
        * score_scale
    )
    full_out = jnp.einsum(
        "ghrt,thd->grhd", full_w.astype(jnp.bfloat16), v_flat, preferred_element_type=jnp.float32
    )
    return attended.at[global_ids].set(full_out.astype(jnp.bfloat16))


def backward_pass(
    q_blocks, k_blocks, v_blocks, out_blocks, d_blocks, slot_ids, usable_t, global_ids, score_scale
):
    block_count, block_len, head_count, head_dim = q_blocks.shape
    group_len, step_count = group_layout(block_count, block_len)
    row_dot = jnp.sum(d_blocks.astype(jnp.float32) * out_blocks.astype(jnp.float32), axis=3)
    is_global = jnp.any(jnp.arange(block_count)[:, None] == global_ids[None, :], axis=1)
    d_rows = jnp.where(is_global[:, None, None, None], jnp.zeros((), jnp.bfloat16), d_blocks)
    dot_rows = jnp.where(is_global[:, None, None], jnp.zeros((), jnp.float32), row_dot)

    def backward_one_group(running, inputs_now):
        dk_sum, dv_sum = running
        q_group, d_group, dot_group, id_group, usable_group = inputs_now
        k_slots = gather_slots(k_blocks, id_group)
        v_slots = gather_slots(v_blocks, id_group)
        weights = slot_weights(q_group, k_slots, usable_group, block_len, score_scale)
        weights_b = weights.astype(jnp.bfloat16)
        d_weights = jnp.einsum(
            "irhd,ijhd->ihrj", d_group, v_slots, preferred_element_type=jnp.float32
        )
        d_scores = (weights * (d_weights - jnp.transpose(dot_group, (0, 2, 1))[..., None])).astype(
            jnp.bfloat16
        )
        dq_group = (
            jnp.einsum("ihrj,ijhd->irhd", d_scores, k_slots, preferred_element_type=jnp.float32)
            * score_scale
        )
        slot_rows = id_group.shape[0] * id_group.shape[1]
        dk_slots = (
            jnp.einsum("ihrj,irhd->ijhd", d_scores, q_group, preferred_element_type=jnp.float32)
            * score_scale
        ).reshape(slot_rows, block_len, head_count, head_dim)
        dv_slots = jnp.einsum(
            "ihrj,irhd->ijhd", weights_b, d_group, preferred_element_type=jnp.float32
        ).reshape(slot_rows, block_len, head_count, head_dim)
        flat_ids = id_group.reshape(-1)
        return ((dk_sum.at[flat_ids].add(dk_slots), dv_sum.at[flat_ids].add(dv_slots)), dq_group)

    empty = jnp.zeros((block_count, block_len, head_count, head_dim), jnp.float32)
    split_inputs = (
        q_blocks.reshape(step_count, group_len, block_len, head_count, head_dim),
        d_rows.reshape(step_count, group_len, block_len, head_count, head_dim),
        dot_rows.reshape(step_count, group_len, block_len, head_count),
        slot_ids.reshape(step_count, group_len, -1),
        usable_t.reshape(step_count, group_len, head_count, -1),
    )
    (dk_blocks, dv_blocks), dq_blocks = lax.scan(backward_one_group, (empty, empty), split_inputs)
    dq_blocks = dq_blocks.reshape(block_count, block_len, head_count, head_dim)
    length = block_count * block_len
    flat_shape = (length, head_count, head_dim)
    k_flat = k_blocks.reshape(flat_shape)
    v_flat = v_blocks.reshape(flat_shape)
    q_global = q_blocks[global_ids]
    d_global = d_blocks[global_ids]
    full_w = softmax_rows(
        jnp.einsum("grhd,thd->ghrt", q_global, k_flat, preferred_element_type=jnp.float32)
        * score_scale
    )
    full_b = full_w.astype(jnp.bfloat16)
    d_full = jnp.einsum("grhd,thd->ghrt", d_global, v_flat, preferred_element_type=jnp.float32)
    full_scores = (
        full_w * (d_full - jnp.transpose(row_dot[global_ids], (0, 2, 1))[..., None])
    ).astype(jnp.bfloat16)
    dq_blocks = dq_blocks.at[global_ids].add(
        jnp.einsum("ghrt,thd->grhd", full_scores, k_flat, preferred_element_type=jnp.float32)
        * score_scale
    )
    dq_all = dq_blocks.reshape(flat_shape)
    dk_all = (
        dk_blocks.reshape(flat_shape)
        + jnp.einsum("ghrt,grhd->thd", full_scores, q_global, preferred_element_type=jnp.float32)
        * score_scale
    )
    dv_all = dv_blocks.reshape(flat_shape) + jnp.einsum(
        "ghrt,grhd->thd", full_b, d_global, preferred_element_type=jnp.float32
    )
    return (dq_all, dk_all, dv_all)


def on_device(queries, keys, values, d_out, gains, window_widths, global_blocks, random_blocks):
    head_count = window_widths.shape[0]
    width_dev = head_count * HD
    global_ids = global_blocks[0]
    random_ids = random_blocks[0]
    block_count = random_ids.shape[0]
    score_scale = 1.0 / math.sqrt(HD)
    all_gains = lax.all_gather(gains, "dp", axis=1, tiled=True)
    own_gains = lax.dynamic_slice_in_dim(all_gains, lax.axis_index("ctx") * width_dev, width_dev, 1)
    gain_q = own_gains[0].reshape(head_count, HD)
    gain_k = own_gains[1].reshape(head_count, HD)
    q_heads, k_heads, v_heads = (
        lax.all_to_all(queries[0], "ctx", split_axis=1, concat_axis=0, tiled=True),
        lax.all_to_all(keys[0], "ctx", split_axis=1, concat_axis=0, tiled=True),
        lax.all_to_all(values[0], "ctx", split_axis=1, concat_axis=0, tiled=True),
    )
    length = q_heads.shape[0]
    block_len = length // block_count
    flat_shape = (length, head_count, HD)
    block_shape = (block_count, block_len, head_count, HD)
    q_scaled = (q_heads.reshape(flat_shape).astype(jnp.float32) * gain_q).astype(jnp.bfloat16)
    k_scaled = (k_heads.reshape(flat_shape).astype(jnp.float32) * gain_k).astype(jnp.bfloat16)
    slot_ids, usable = slot_table(global_ids, random_ids, window_widths)
    usable_t = jnp.transpose(usable, (1, 0, 2))
    out_blocks = forward_pass(
        q_scaled.reshape(block_shape),
        k_scaled.reshape(block_shape),
        v_heads.reshape(block_shape),
        slot_ids,
        usable_t,
        global_ids,
        score_scale,
    )
    out_tokens = lax.all_to_all(
        out_blocks.reshape(length, width_dev), "ctx", split_axis=0, concat_axis=1, tiled=True
    )
    d_heads = lax.all_to_all(d_out[0], "ctx", split_axis=1, concat_axis=0, tiled=True)
    q_back, k_back, v_back = (q_heads, k_heads, v_heads)
    q_back_scaled, k_back_scaled = (q_scaled, k_scaled)
    dq_all, dk_all, dv_all = backward_pass(
        q_back_scaled.reshape(block_shape),
        k_back_scaled.reshape(block_shape),
        v_back.reshape(block_shape),
        out_blocks,
        d_heads.reshape(block_shape),
        slot_ids,
        usable_t,
        global_ids,
        score_scale,
    )
    grad_q = (dq_all * gain_q).astype(jnp.bfloat16).reshape(length, width_dev)
    grad_k = (dk_all * gain_k).astype(jnp.bfloat16).reshape(length, width_dev)
    grad_v = dv_all.astype(jnp.bfloat16).reshape(length, width_dev)
    back_q, back_k, back_v = (
        lax.all_to_all(grad_q, "ctx", split_axis=0, concat_axis=1, tiled=True),
        lax.all_to_all(grad_k, "ctx", split_axis=0, concat_axis=1, tiled=True),
        lax.all_to_all(grad_v, "ctx", split_axis=0, concat_axis=1, tiled=True),
    )
    gain_terms = jnp.stack(
        [
            jnp.sum(dq_all * q_back.reshape(flat_shape).astype(jnp.float32), axis=0),
            jnp.sum(dk_all * k_back.reshape(flat_shape).astype(jnp.float32), axis=0),
        ]
    ).reshape(2, width_dev)
    columns = lax.all_gather(gain_terms, "ctx", axis=1, tiled=True)
    d_gains = lax.psum_scatter(
        columns.astype(jnp.bfloat16), "dp", scatter_dimension=1, tiled=True
    ).astype(jnp.float32)
    return (out_tokens[None], back_q[None], back_k[None], back_v[None], d_gains)


def solution(mesh):
    placed = (
        P("dp", "ctx", None),
        P("dp", "ctx", None),
        P("dp", "ctx", None),
        P("dp", "ctx", None),
        P(None, "dp"),
        P("ctx"),
        P("dp", None),
        P("dp", None, None),
    )
    return jax.shard_map(
        on_device,
        mesh=mesh,
        in_specs=placed,
        out_specs=(
            P("dp", "ctx", None),
            P("dp", "ctx", None),
            P("dp", "ctx", None),
            P("dp", "ctx", None),
            P(None, "dp"),
        ),
        check_vma=False,
    )
```

profile of v0, /device:TPU:1, one launch (start us, length us, event | category | flops | bytes accessed | tf_op | source)
XLA Modules:
  0.0 672.8 jit_solution(1531738499549589078)
XLA Ops:
  10.1 8.6 %all-to-all-start.1 = ((bf16[128,32,128]{2,0,1:T(8,128)(2,1)}), bf16[128,32,128]{2,0,1:T(8,128)(2,1)S(1)}, u32[]{:S(2)}, u32[]{:S(2)}) async-start(bf16[128,32,128]{2,0,1:T(8,128)(2,1)} %copy.222), calls=%async_computation.1 | async-start | bytes 2097152 | tf_op jit(solution)/shard_map/all_to_all | solution.py:192
  20.0 15.6 %all-to-all-done.1 = bf16[128,32,128]{2,0,1:T(8,128)(2,1)S(1)} async-done(((bf16[128,32,128]{2,0,1:T(8,128)(2,1)}), bf16[128,32,128]{2,0,1:T(8,128)(2,1)S(1)}, u32[]{:S(2)}, u32[]{:S(2)}) %all-to-all-start.1) | async-done | bytes 1048608 | tf_op jit(solution)/shard_map/all_to_all | solution.py:192
  35.6 4.1 all-to-all-start.2
  42.1 14.6 %all-to-all-done.2 = bf16[128,32,128]{0,2,1:T(8,128)(2,1)S(1)} async-done(((bf16[128,32,128]{0,2,1:T(8,128)(2,1)}), bf16[128,32,128]{0,2,1:T(8,128)(2,1)S(1)}, u32[]{:S(2)}, u32[]{:S(2)}) %all-to-all-start.2) | async-done | bytes 1048608 | tf_op jit(solution)/shard_map/all_to_all | solution.py:193
  56.6 4.0 all-to-all-start
  66.5 11.0 %all-to-all-done = bf16[128,32,128]{0,2,1:T(8,128)(2,1)S(1)} async-done(((bf16[128,32,128]{0,2,1:T(8,128)(2,1)}), bf16[128,32,128]{0,2,1:T(8,128)(2,1)S(1)}, u32[]{:S(2)}, u32[]{:S(2)}) %all-to-all-start) | async-done | bytes 1048608 | tf_op jit(solution)/shard_map/all_to_all | solution.py:194
  78.5 4.0 all-to-all-start.4
  82.5 23.1 %all_gather.6 = f32[2,4096]{1,0:T(2,128)S(1)} all-gather(f32[2,512]{1,0:T(2,128)S(1)} %copy-done.23), channel_id=1, replica_groups=mesh['dp'=8,'ctx'=32] {'dp'}, dimensions={1}, use_global_device_ids=true | all-gather | bytes 36864 | tf_op jit(solution)/shard_map/all_gather | solution.py:187
  121.6 76.6 %while.24 = (s32[]{:T(128)}, bf16[8,4,128,1,128]{4,2,1,0,3:T(8,128)(2,1)}, s32[8,4,8]{2,1,0:T(4,128)S(1)}, bf16[32,128,1,128]{3,1,0,2:T(8,128)(2,1)S(1)}, pred[8...) while((s32[]{:T(128)}, ...), condition=%wide.region_4.5_spmd, body=%wide.region_1.4_spmd.sunk | while | flops 271648864 | bytes 11297869 | solution.py:85
  209.1 3.4 fusion.56
  220.0 292.3 %while.25 = (s32[]{:T(128)}, f32[32,128,1,128]{3,1,0,2:T(8,128)}, f32[32,128,1,128]{3,1,0,2:T(8,128)}, f32[8,4,128,1,128]{4,2,1,0,3:T(8,128)}, s32[8,4,8]{2,1,0:...) while((s32[]{:T(128)}, f32[32,128,1,128]{3,1,0,2:T(8,128)}, ...), condition=%wide.region_15.16_spmd, body=%wide.region_10.15_spmd.sunk | while | flops 677972160 | bytes 57460872 | solution.py:147
  237.3 6.4 scatter_fusion.1
  244.5 3.1 multiply_bitcast_fusion.2
  249.5 6.3 scatter_fusion
  261.5 3.0 fusion.144
  273.8 6.3 scatter_fusion.1
  281.0 3.1 multiply_bitcast_fusion.2
  286.0 6.3 scatter_fusion
  310.4 6.4 scatter_fusion.1
  317.6 3.1 multiply_bitcast_fusion.2
  322.7 6.3 scatter_fusion
  347.0 6.3 scatter_fusion.1
  354.2 3.1 multiply_bitcast_fusion.2
  359.2 6.4 scatter_fusion
  383.6 6.3 scatter_fusion.1
  390.7 3.1 multiply_bitcast_fusion.2
  395.8 6.4 scatter_fusion
  420.2 6.2 scatter_fusion.1
  427.2 3.1 multiply_bitcast_fusion.2
  432.3 6.3 scatter_fusion
  456.6 6.3 scatter_fusion.1
  463.7 3.1 multiply_bitcast_fusion.2
  468.8 6.4 scatter_fusion
  480.9 3.0 fusion.144
  493.2 6.2 scatter_fusion.1
  500.2 3.1 multiply_bitcast_fusion.2
  505.3 6.3 scatter_fusion
  517.2 29.5 %all_to_all.119 = bf16[32,128,128]{2,1,0:T(8,128)(2,1)} all-to-all(bf16[32,128,128]{2,1,0:T(8,128)(2,1)S(1)} %get-tuple-element.281), channel_id=1, replica_groups=mesh['dp'=8,'ctx'=32] {'ctx'}, dimensions={0} | all-to-all | bytes 2097152 | tf_op jit(solution)/shard_map/all_to_all | solution.py:234
  546.7 4.0 all-to-all-start.3
  555.9 3.1 copy.271
  559.0 3.2 multiply_reduce_fusion.1
  563.9 3.7 all-to-all-done.3
  567.5 4.7 all-to-all-start.6
  572.3 3.1 copy.272
  579.4 9.5 %all-to-all-done.6 = bf16[32,128,128]{1,2,0:T(8,128)(2,1)} async-done(((bf16[32,128,128]{1,2,0:T(8,128)(2,1)}), bf16[32,128,128]{1,2,0:T(8,128)(2,1)}, u32[]{:S(2)}, u32[]{:S(2)}) %all-to-all-start.6) | async-done | bytes 1048608 | tf_op jit(solution)/shard_map/all_to_all | solution.py:235
  589.0 3.9 all-to-all-start.7
  593.0 29.8 %all-gather = bf16[2,1,4096]{2,1,0:T(2,128)(2,1)S(1)} all-gather(bf16[2,1,128]{2,1,0:T(2,128)(2,1)S(1)} %pad_maximum_fusion), channel_id=2, replica_groups=mesh['dp'=8,'ctx'=32] {'ctx'}, dimensions={2}, use_global_device_ids=true | all-gather | bytes 16896 | tf_op jit(solution)/shard_map/all_gather | solution.py:244
  624.2 31.1 %reduce-scatter.4.cloned.1.call-done = bf16[512,2]{1,0:T(8,128)(2,1)} async-done(((bf16[4096,2]{1,0:T(8,128)(2,1)}), bf16[512,2]{1,0:T(8,128)(2,1)}) %reduce-scatter.4.cloned.1.call-update) | async-done | bytes 2064
  (451 shorter events, 310.8 us)
Async XLA Ops:
  8.8 9.9 %copy-start.16 = (bf16[1,128,4096]{2,1,0:T(8,128)(2,1)S(1)}, bf16[1,128,4096]{2,1,0:T(8,128)(2,1)}, u32[]{:S(2)}) copy-start(bf16[1,128,4096]{2,1,0:T(8,128)(2,1)} %param.13) | copy-start | bytes 3145732
  10.1 25.5 %all-to-all-start.1 = ((bf16[128,32,128]{2,0,1:T(8,128)(2,1)}), bf16[128,32,128]{2,0,1:T(8,128)(2,1)S(1)}, u32[]{:S(2)}, u32[]{:S(2)}) async-start(bf16[128,32,128]{2,0,1:T(8,128)(2,1)} %copy.222), calls=%async_computation.1 | async-start | bytes 2097152 | tf_op jit(solution)/shard_map/all_to_all | solution.py:192
  18.7 21.7 %copy-start.21 = (s32[1,32,3]{1,0,2:T(1,128)S(1)}, s32[1,32,3]{1,0,2:T(1,128)}, u32[]{:S(2)}) copy-start(s32[1,32,3]{1,0,2:T(1,128)} %param.19) | copy-start | bytes 1156
  20.0 20.4 %copy-start.17 = (bf16[1,128,4096]{2,1,0:T(8,128)(2,1)S(1)}, bf16[1,128,4096]{2,1,0:T(8,128)(2,1)}, u32[]{:S(2)}) copy-start(bf16[1,128,4096]{2,1,0:T(8,128)(2,1)} %param.14) | copy-start | bytes 3145732
  35.6 75.2 %copy-start.8 = (bf16[128,32,128]{2,0,1:T(8,128)(2,1)}, bf16[128,32,128]{2,0,1:T(8,128)(2,1)S(1)}, u32[]{:S(2)}) copy-start(bf16[128,32,128]{2,0,1:T(8,128)(2,1)S(1)} %all-to-all-done.1) | copy-start | bytes 3145732
  35.6 6.3 copy-start.24
  35.6 21.0 %all-to-all-start.2 = ((bf16[128,32,128]{0,2,1:T(8,128)(2,1)}), bf16[128,32,128]{0,2,1:T(8,128)(2,1)S(1)}, u32[]{:S(2)}, u32[]{:S(2)}) async-start(bf16[128,32,128]{0,2,1:T(8,128)(2,1)} %bitcast.47), calls=%async_computation.2 | async-start | bytes 2097152 | tf_op jit(solution)/shard_map/all_to_all | solution.py:193
  56.6 48.9 %copy-start.11 = (bf16[128,32,128]{0,2,1:T(8,128)(2,1)}, bf16[128,32,128]{0,2,1:T(8,128)(2,1)S(1)}, u32[]{:S(2)}) copy-start(bf16[128,32,128]{0,2,1:T(8,128)(2,1)S(1)} %all-to-all-done.2) | copy-start | bytes 3145732
  56.6 20.9 %all-to-all-start = ((bf16[128,32,128]{0,2,1:T(8,128)(2,1)}), bf16[128,32,128]{0,2,1:T(8,128)(2,1)S(1)}, u32[]{:S(2)}, u32[]{:S(2)}) async-start(bf16[128,32,128]{0,2,1:T(8,128)(2,1)} %bitcast.378), calls=%async_computation | async-start | bytes 2097152 | tf_op jit(solution)/shard_map/all_to_all | solution.py:194
  64.2 18.2 %copy-start.23 = (f32[2,512]{1,0:T(2,128)S(1)}, f32[2,512]{1,0:T(2,128)}, u32[]{:S(2)}) copy-start(f32[2,512]{1,0:T(2,128)} %param.16) | copy-start | bytes 12292
  66.5 138.2 %copy-start.22 = (s32[2]{0:T(128)}, s32[2]{0:T(128)S(1)}, u32[]{:S(2)}) copy-start(s32[2]{0:T(128)S(1)} %fusion.87) | copy-start | bytes 28
  78.5 35.4 %all-to-all-start.4 = ((bf16[128,32,128]{2,0,1:T(8,128)(2,1)}), bf16[128,32,128]{2,0,1:T(8,128)(2,1)S(1)}, u32[]{:S(2)}, u32[]{:S(2)}) async-start(bf16[128,32,128]{2,0,1:T(8,128)(2,1)} %copy.234), calls=%async_computation.4 | async-start | bytes 2097152 | tf_op jit(solution)/shard_map/all_to_all | solution.py:216
  105.6 14.8 %copy-start.20 = (f32[128]{0:T(128)}, f32[128]{0:T(128)S(1)}, u32[]{:S(2)}) copy-start(f32[128]{0:T(128)S(1)} %get-tuple-element.285) | copy-start | bytes 1540
  105.6 106.9 %copy-start.18 = (f32[128]{0:T(128)}, f32[128]{0:T(128)S(1)}, u32[]{:S(2)}) copy-start(f32[128]{0:T(128)S(1)} %get-tuple-element.284) | copy-start | bytes 1540
  116.9 2.0 copy-start.5
  203.4 3.3 copy-start.10
  209.1 4.8 copy-start.7
  230.6 2.0 copy-start.25
  230.6 2.0 copy-start.27
  249.5 6.3 copy-start.4
  267.2 2.0 copy-start.25
  267.2 2.0 copy-start.27
  286.0 6.3 copy-start.4
  303.7 2.0 copy-start.25
  303.7 2.0 copy-start.27
  322.7 6.3 copy-start.4
  340.4 2.0 copy-start.25
  340.4 2.0 copy-start.27
  359.2 6.4 copy-start.4
  377.0 2.0 copy-start.25
  377.0 2.0 copy-start.27
  395.8 6.4 copy-start.4
  413.5 2.0 copy-start.25
  413.5 2.0 copy-start.27
  432.3 6.4 copy-start.4
  450.0 2.0 copy-start.25
  468.8 6.4 copy-start.4
  486.6 2.0 copy-start.25
  505.3 6.3 copy-start.4
  517.2 33.4 %copy-start.6 = (f32[32,128,128]{1,2,0:T(8,128)S(1)}, f32[32,128,128]{1,2,0:T(8,128)}, u32[]{:S(2)}) copy-start(f32[32,128,128]{1,2,0:T(8,128)} %copy-done.5) | copy-start | bytes 6291460
  546.7 20.9 %all-to-all-start.3 = ((bf16[32,128,128]{2,1,0:T(8,128)(2,1)}), bf16[32,128,128]{2,1,0:T(8,128)(2,1)S(1)}, u32[]{:S(2)}, u32[]{:S(2)}) async-start(bf16[32,128,128]{2,1,0:T(8,128)(2,1)} %scatter_fusion.2), calls=%async_computation.3 | async-start | bytes 2097152 | tf_op jit(solution)/shard_map/all_to_all | solution.py:213
  555.9 3.1 copy-start.13
  555.9 3.1 copy-start.19
  567.5 21.4 %all-to-all-start.6 = ((bf16[32,128,128]{1,2,0:T(8,128)(2,1)}), bf16[32,128,128]{1,2,0:T(8,128)(2,1)}, u32[]{:S(2)}, u32[]{:S(2)}) async-start(bf16[32,128,128]{1,2,0:T(8,128)(2,1)} %copy.248), calls=%async_computation.6 | async-start | bytes 2097152 | tf_op jit(solution)/shard_map/all_to_all | solution.py:235
  572.3 3.1 copy-start.3
  579.4 77.4 %copy-start.14 = (bf16[32,128,128]{2,1,0:T(8,128)(2,1)S(1)}, bf16[32,128,128]{2,1,0:T(8,128)(2,1)}, u32[]{:S(2)}) copy-start(bf16[32,128,128]{2,1,0:T(8,128)(2,1)} %all_to_all.119) | copy-start | bytes 3145732
  589.0 75.7 %all-to-all-start.7 = ((bf16[32,128,128]{1,2,0:T(8,128)(2,1)}), bf16[32,128,128]{1,2,0:T(8,128)(2,1)S(1)}, u32[]{:S(2)}, u32[]{:S(2)}) async-start(bf16[32,128,128]{1,2,0:T(8,128)(2,1)} %copy.252), calls=%async_computation.7 | async-start | bytes 2097152 | tf_op jit(solution)/shard_map/all_to_all | solution.py:236
  592.9 62.4 %reduce-scatter.4.cloned.1.call-start = ((), (), s32[]{:S(2)}) async-start(), calls=%async_computation.9 | async-start | bytes 1179648
  (23 other events, 22.8 us)
Sparse Core Ops, SparseCore 0:
  624.3 30.9 reduce-scatter.3
where the time goes:
time: 683 us; the launch traced here: 673 us
  local copies, waits for them, and re-layouts  185 us (27%)
  matrix products  147 us (22%)
  other arithmetic  124 us (18%)
  waiting for transfers between devices  85.5 us (13%)
  blocking collectives  82.3 us (12%)
  starting transfers between devices  33.2 us (5%)
  between operations  15.1 us (2%)
    scatter-add x8, other arithmetic, backward_one_group(): dk_sum.at[flat_ids].add(dk_slots)  50.8 us
    scatter-add x8, other arithmetic, backward_one_group(): dv_sum.at[flat_ids].add(dv_slots)  50.3 us
    sub x16, matrix products, softmax_rows(): exponent = jnp.exp(scores - row_max)  47.9 us
    gather x32, local copies, waits for them, and re-layouts, gather_slots(): picked = blocks_in[id_group]  43.5 us
    unnamed x2, waiting for transfers between devices  31.1 us
    all_gather x1, blocking collectives, on_device(): columns = lax.all_gather(gain_terms, 'ctx', axis=1, tiled=True)  29.8 us
    all_to_all x1, blocking collectives, on_device(): lax.all_to_all(grad_q, 'ctx', split_axis=0, concat_axis=1, tiled=True)  29.5 us
    dot_general x8, matrix products, backward_one_group(): jnp.einsum('ihrj,irhd->ijhd', d_scores, q_group, preferred_element_type=j...  25.1 us
  transfers between devices with their start and end apart: 8, of which 6 were waited for; matrix products, arithmetic and copies ran while one was open for 7% of the time, Pallas kernels for 0%

commit v1 on v0

v1 whole, which is shorter than its diff:
```python
import functools
import math

import jax
import jax.numpy as jnp
from jax import lax
from jax.experimental import pallas as pl
from jax.experimental.pallas import tpu as pltpu
from jax.sharding import PartitionSpec as P

HD = 128
BLOCK = 128
SCALE = 1.0 / math.sqrt(HD)
SCALE_LOG2 = SCALE * math.log2(math.e)
PENALTY = 1e30
CHUNK = 4
F32 = jnp.float32
BF16 = jnp.bfloat16


def dot_nn(a, b):
    return lax.dot_general(a, b, (((1,), (0,)), ((), ())), preferred_element_type=F32)


def dot_nt(a, b):
    return lax.dot_general(a, b, (((1,), (1,)), ((), ())), preferred_element_type=F32)


def dot_tn(a, b):
    return lax.dot_general(a, b, (((0,), (0,)), ((), ())), preferred_element_type=F32)


def lane_fold(combine, wide):
    folded = wide[:, :128]
    for n in range(1, wide.shape[1] // 128):
        folded = combine(folded, wide[:, n * 128 : (n + 1) * 128])
    return folded


def attention_kernel(
    width_ref, global_ref, random_ref, x_ref, gain_ref, y_ref, terms_ref,
    ks_ref, p_ref, dk_ref, dv_ref, tq_ref,
):
    block_count = x_ref.shape[0]
    chunk_count = block_count // CHUNK
    gain_q = gain_ref[0:1, :]
    gain_k = gain_ref[1:2, :]
    g0 = global_ref[0, 0]
    g1 = global_ref[0, 1]
    wide = width_ref[0] >= 1
    low = jnp.minimum(g0, g1)
    high = jnp.maximum(g0, g1)

    def scale_keys(j, carry):
        ks_ref[j] = (x_ref[j, 1].astype(F32) * gain_k).astype(BF16)
        return carry

    lax.fori_loop(0, block_count, scale_keys, 0, unroll=4)

    q_raw = jnp.concatenate([x_ref[g0, 0], x_ref[g1, 0]], 0).astype(F32)
    q_scaled = (q_raw * gain_q).astype(BF16)
    d_out = jnp.concatenate([x_ref[g0, 3], x_ref[g1, 3]], 0)
    rows = 2 * BLOCK

    def key_chunk(c):
        return ks_ref[pl.ds(c * CHUNK, CHUNK)].reshape(CHUNK * BLOCK, HD)

    def value_chunk(c):
        return x_ref[pl.ds(c * CHUNK, CHUNK), 2].reshape(CHUNK * BLOCK, HD)

    def full_scores(c, top):
        scores = dot_nt(q_scaled, key_chunk(c))
        p_ref[c] = scores
        return jnp.maximum(top, lane_fold(jnp.maximum, scores))

    top = lax.fori_loop(0, chunk_count, full_scores, jnp.full((rows, 128), -3e38, F32))
    top = jnp.max(top, axis=1, keepdims=True) * SCALE_LOG2

    def full_exp(c, total):
        e = jnp.exp2(p_ref[c] * SCALE_LOG2 - top)
        p_ref[c] = e
        return total + lane_fold(jnp.add, e)

    total = lax.fori_loop(0, chunk_count, full_exp, jnp.zeros((rows, 128), F32))
    inverse = 1.0 / jnp.sum(total, axis=1, keepdims=True)

    def full_out(c, acc):
        p = p_ref[c] * inverse
        p_ref[c] = p
        p_b = p.astype(BF16)
        dv_t = dot_tn(d_out, p_b)
        for n in range(CHUNK):
            dv_ref[c * CHUNK + n] = dv_t[:, n * 128 : (n + 1) * 128]
        return acc + dot_nn(p_b, value_chunk(c))

    out = lax.fori_loop(0, chunk_count, full_out, jnp.zeros((rows, HD), F32)).astype(BF16)
    y_ref[g0, 0] = out[:BLOCK]
    y_ref[g1, 0] = out[BLOCK:]
    row_dot = jnp.sum(d_out.astype(F32) * out.astype(F32), axis=1, keepdims=True)

    def full_back(c, acc):
        dp = dot_nt(d_out, value_chunk(c))
        ds = (p_ref[c] * (dp - row_dot)).astype(BF16)
        dk_t = dot_tn(q_scaled, ds)
        for n in range(CHUNK):
            dk_ref[c * CHUNK + n] = dk_t[:, n * 128 : (n + 1) * 128]
        return acc + dot_nn(ds, key_chunk(c))

    dq = lax.fori_loop(0, chunk_count, full_back, jnp.zeros((rows, HD), F32)) * SCALE
    dq_b = (dq * gain_q).astype(BF16)
    y_ref[g0, 1] = dq_b[:BLOCK]
    y_ref[g1, 1] = dq_b[BLOCK:]
    terms = dq * q_raw
    tq_ref[...] = terms[:BLOCK] + terms[BLOCK:]

    def sparse_block(i):
        ids = [i]
        penalties = [jnp.float32(0.0)]
        candidates = [(i - 1, wide & (i > 0)), (i + 1, wide & (i < block_count - 1))]
        candidates += [(g0, None), (g1, None)]
        candidates += [(random_ref[0, i, n], None) for n in range(random_ref.shape[2])]
        for block_id, listed in candidates:
            unusable = functools.reduce(jnp.logical_or, [block_id == t for t in ids])
            if listed is not None:
                unusable = unusable | jnp.logical_not(listed)
            ids.append(jnp.where(unusable, i, block_id))
            penalties.append(jnp.where(unusable, jnp.float32(PENALTY), jnp.float32(0.0)))
        slots = len(ids)
        k_slots = jnp.concatenate([ks_ref[t] for t in ids], 0)
        v_slots = jnp.concatenate([x_ref[t, 2] for t in ids], 0)
        q_raw = x_ref[i, 0].astype(F32)
        q_scaled = (q_raw * gain_q).astype(BF16)
        d_out = x_ref[i, 3]
        scores = dot_nt(q_scaled, k_slots)
        dp = dot_nt(d_out, v_slots)
        top = jnp.max(lane_fold(jnp.maximum, scores), axis=1, keepdims=True) * SCALE_LOG2
        es = [
            jnp.exp2(scores[:, t * 128 : (t + 1) * 128] * SCALE_LOG2 - (top + penalties[t]))
            for t in range(slots)
        ]
        inverse = 1.0 / jnp.sum(functools.reduce(jnp.add, es), axis=1, keepdims=True)
        p = jnp.concatenate([e * inverse for e in es], 1)
        p_b = p.astype(BF16)
        out = dot_nn(p_b, v_slots).astype(BF16)
        y_ref[i, 0] = out
        row_dot = jnp.sum(d_out.astype(F32) * out.astype(F32), axis=1, keepdims=True)
        ds = (p * (dp - row_dot)).astype(BF16)
        dq = dot_nn(ds, k_slots) * SCALE
        y_ref[i, 1] = (dq * gain_q).astype(BF16)
        tq_ref[...] += dq * q_raw
        dv_t = dot_tn(d_out, p_b)
        dk_t = dot_tn(q_scaled, ds)
        for t in range(slots):
            dv_ref[ids[t]] += dv_t[:, t * 128 : (t + 1) * 128]
        for t in range(slots):
            dk_ref[ids[t]] += dk_t[:, t * 128 : (t + 1) * 128]

    def step(n, carry):
        i = n + (n >= low).astype(jnp.int32)
        i = i + (i >= high).astype(jnp.int32)
        sparse_block(i)
        return carry

    lax.fori_loop(0, block_count - 2, step, 0)

    def finish(j, acc):
        dk = dk_ref[j].T * SCALE
        y_ref[j, 2] = (dk * gain_k).astype(BF16)
        y_ref[j, 3] = dv_ref[j].T.astype(BF16)
        return acc + dk * x_ref[j, 1].astype(F32)

    tk = lax.fori_loop(0, block_count, finish, jnp.zeros((BLOCK, HD), F32))
    terms_ref[0:1, :] = jnp.sum(tq_ref[...], axis=0, keepdims=True)
    terms_ref[1:2, :] = jnp.sum(tk, axis=0, keepdims=True)


def attention(widths, global_ids, random_ids, x, gains):
    block_count = x.shape[0]
    smem = pl.BlockSpec(memory_space=pltpu.SMEM)
    vmem = pl.BlockSpec(memory_space=pltpu.VMEM)
    return pl.pallas_call(
        attention_kernel,
        out_shape=(
            jax.ShapeDtypeStruct((block_count, 4, BLOCK, HD), BF16),
            jax.ShapeDtypeStruct((2, HD), F32),
        ),
        in_specs=[smem, smem, smem, vmem, vmem],
        out_specs=(vmem, vmem),
        scratch_shapes=[
            pltpu.VMEM((block_count, BLOCK, HD), BF16),
            pltpu.VMEM((block_count // CHUNK, 2 * BLOCK, CHUNK * BLOCK), F32),
            pltpu.VMEM((block_count, HD, BLOCK), F32),
            pltpu.VMEM((block_count, HD, BLOCK), F32),
            pltpu.VMEM((BLOCK, HD), F32),
        ],
        compiler_params=pltpu.CompilerParams(vmem_limit_bytes=40 * 1024 * 1024),
        name="attention",
    )(widths, global_ids, random_ids, x, gains)


HEADS_A_STEP = 8


def split_kernel(q_ref, k_ref, v_ref, d_ref, x_ref):
    for n, ref in enumerate((q_ref, k_ref, v_ref, d_ref)):
        for h in range(HEADS_A_STEP):
            x_ref[h, n] = ref[0, :, h * HD : (h + 1) * HD]


def split_heads(arrays):
    _, tokens, channels = arrays[0].shape
    heads = channels // HD
    spec = pl.BlockSpec((1, tokens, HEADS_A_STEP * HD), lambda i: (0, 0, i))
    return pl.pallas_call(
        split_kernel,
        grid=(heads // HEADS_A_STEP,),
        out_shape=jax.ShapeDtypeStruct((heads, 4, tokens, HD), BF16),
        in_specs=[spec] * 4,
        out_specs=pl.BlockSpec((HEADS_A_STEP, 4, tokens, HD), lambda i: (i, 0, 0, 0)),
        compiler_params=pltpu.CompilerParams(vmem_limit_bytes=24 * 1024 * 1024),
        name="split_heads",
    )(*arrays)


def join_kernel(y_ref, o_ref, q_ref, k_ref, v_ref):
    for n, ref in enumerate((o_ref, q_ref, k_ref, v_ref)):
        for h in range(HEADS_A_STEP):
            ref[0, :, h * HD : (h + 1) * HD] = y_ref[h, n]


def join_heads(y):
    heads, _, tokens, _ = y.shape
    spec = pl.BlockSpec((1, tokens, HEADS_A_STEP * HD), lambda i: (0, 0, i))
    return pl.pallas_call(
        join_kernel,
        grid=(heads // HEADS_A_STEP,),
        out_shape=(jax.ShapeDtypeStruct((1, tokens, heads * HD), BF16),) * 4,
        in_specs=[pl.BlockSpec((HEADS_A_STEP, 4, tokens, HD), lambda i: (i, 0, 0, 0))],
        out_specs=(spec,) * 4,
        compiler_params=pltpu.CompilerParams(vmem_limit_bytes=24 * 1024 * 1024),
        name="join_heads",
    )(y)


def exchange(x):
    return lax.all_to_all(x, "ctx", split_axis=0, concat_axis=0, tiled=True)


def on_device(queries, keys, values, d_out, gains, window_widths, global_blocks, random_blocks):
    x = exchange(split_heads((queries, keys, values, d_out)))
    all_gains = lax.all_gather(gains, "dp", axis=1, tiled=True)
    own_gains = lax.dynamic_slice_in_dim(all_gains, lax.axis_index("ctx") * HD, HD, 1)
    y, terms = attention(window_widths, global_blocks, random_blocks, x, own_gains)
    out, d_queries, d_keys, d_values = join_heads(exchange(y))
    head_terms = lax.psum(terms, "dp")
    columns = lax.all_gather(head_terms, "ctx", axis=1, tiled=True)
    own_width = gains.shape[1]
    d_gains = lax.dynamic_slice_in_dim(columns, lax.axis_index("dp") * own_width, own_width, 1)
    return (out, d_queries, d_keys, d_values, d_gains)


def solution(mesh):
    tokens = P("dp", "ctx", None)
    return jax.shard_map(
        on_device,
        mesh=mesh,
        in_specs=(
            tokens, tokens, tokens, tokens,
            P(None, "dp"), P("ctx"), P("dp", None), P("dp", None, None),
        ),
        out_specs=(tokens, tokens, tokens, tokens, P(None, "dp")),
        check_vma=False,
    )
```

time: 683 us -> 199 us (0.29); the launches traced: 673 us -> 199 us
  local copies, waits for them, and re-layouts: 185 us -> 9.5 us
  matrix products: 147 us -> 0 us
  other arithmetic: 124 us -> 0 us
  waiting for transfers between devices: 85.5 us -> 27.2 us
  Pallas kernels: 0 us -> 53.1 us
  starting transfers between devices: 33.2 us -> 15.9 us
  between operations: 15.1 us -> 1.37 us
  blocking collectives: 82.3 us -> 91.5 us
    scatter-add x17 -> x0, other arithmetic: 103 us -> none  [the longest x8 50.8 us: backward_one_group(): dk_sum.at[flat_ids].add(dk_slots)]
    dot_general x46 -> x0, matrix products: 98.7 us -> none  [the longest x8 25.1 us: backward_one_group(): jnp.einsum('ihrj,irhd->ijhd', d_scores, q_group, preferred_element_type=j...]
    pallas_call x0 -> x3, Pallas kernels: none -> 53.1 us  [the longest x1 46.9 us: attention(): pl.pallas_call(attention_kernel, out_shape=(jax.ShapeDtypeStruct((block_c...]
    sub x16 -> x0, matrix products: 47.9 us -> none  [softmax_rows(): exponent = jnp.exp(scores - row_max)]
    gather x35 -> x0, local copies, waits for them, and re-layouts: 46.5 us -> none  [the longest x32 43.5 us: gather_slots(): picked = blocks_in[id_group]]
    unnamed x2 -> x0, waiting for transfers between devices: 31.1 us -> none
    all_to_all x1 -> x0, blocking collectives: 29.5 us -> none  [on_device(): lax.all_to_all(grad_q, 'ctx', split_axis=0, concat_axis=1, tiled=True)]
    all_to_all x7 -> x2, waiting for transfers between devices: 54.4 us -> 27.2 us  [exchange(): return lax.all_to_all(x, 'ctx', split_axis=0, concat_axis=0, tiled=True)]
  transfers between devices with their start and end apart: 8 -> 2, of which waited for: 6 -> 1; matrix products, arithmetic and copies ran while one was open for 7% -> 0% of each run, Pallas kernels for 0% -> 0%
where the time goes in v1:
time: 199 us
  blocking collectives  91.5 us (46%)
  Pallas kernels  53.1 us (27%)
  waiting for transfers between devices  27.2 us (14%)
  starting transfers between devices  15.9 us (8%)
  local copies, waits for them, and re-layouts  9.5 us (5%)
    all_gather x1, blocking collectives, on_device(): columns = lax.all_gather(head_terms, 'ctx', axis=1, tiled=True)  49.3 us
    pallas_call x1, Pallas kernels, attention(): pl.pallas_call(attention_kernel, out_shape=(jax.ShapeDtypeStruct((block_c...  46.9 us
    all_to_all x2, waiting for transfers between devices, exchange(): return lax.all_to_all(x, 'ctx', split_axis=0, concat_axis=0, tiled=True)  27.2 us
    all_gather x1, blocking collectives, on_device(): all_gains = lax.all_gather(gains, 'dp', axis=1, tiled=True)  24.3 us
    psum x1, blocking collectives, on_device(): head_terms = lax.psum(terms, 'dp')  17.9 us
    all_to_all x2, starting transfers between devices, exchange(): return lax.all_to_all(x, 'ctx', split_axis=0, concat_axis=0, tiled=True)  15.9 us
    unnamed x19, local copies, waits for them, and re-layouts  8.9 us
    pallas_call x1, Pallas kernels, join_heads(): pl.pallas_call(join_kernel, grid=(heads // HEADS_A_STEP,), out_shape=(jax...  5.09 us
  transfers between devices with their start and end apart: 2, of which 1 were waited for; matrix products, arithmetic and copies ran while one was open for 0% of the time, Pallas kernels for 0%

profile of v1, /device:TPU:1, one launch (start us, length us, event | category | flops | bytes accessed | tf_op | source)
XLA Modules:
  0.0 198.5 jit_solution(12432295195257829380)
XLA Ops:
  0.6 0.0 copy-start.2
  0.6 1.2 copy-done.2
  1.9 0.0 copy-start.3
  1.9 1.2 copy-done.3
  3.1 0.0 copy-start.4
  3.1 1.2 copy-done.4
  4.3 0.0 copy-start.5
  4.3 1.2 copy-done.5
  5.5 1.1 split_heads.1
  6.6 0.0 copy-start
  6.7 2.0 copy-done
  8.6 0.0 copy-start.8
  8.6 0.0 copy-start.7
  8.6 0.0 copy-start.6
  8.6 8.8 %all-to-all-start = ((bf16[32,4,128,128]{3,2,1,0:T(8,128)(2,1)}), bf16[32,4,128,128]{3,2,1,0:T(8,128)(2,1)}, u32[]{:S(2)}, u32[]{:S(2)}) async-start(bf16[32,4,128,128]{3,2,1,0:T(8,128)(2,1)} %copy-done), calls=%async_computation | async-start | bytes 8388608 | tf_op jit(solution)/shard_map/all_to_all | solution.py:246
  17.4 0.0 copy-done.8
  17.4 0.1 copy.13.random_ref
  18.2 0.0 copy-done.7
  18.2 24.3 %all_gather.6 = f32[2,4096]{1,0:T(2,128)S(1)} all-gather(f32[2,512]{1,0:T(2,128)S(1)} %copy-done.7), channel_id=1, replica_groups=mesh['dp'=8,'ctx'=32] {'dp'}, dimensions={1}, use_global_device_ids=true | all-gather | bytes 36864 | tf_op jit(solution)/shard_map/all_gather | solution.py:251
  42.4 27.2 %all-to-all-done.x_ref = bf16[32,4,128,128]{3,2,1,0:T(8,128)(2,1)} async-done(((bf16[32,4,128,128]{3,2,1,0:T(8,128)(2,1)}), bf16[32,4,128,128]{3,2,1,0:T(8,128)(2,1)}, u32[]{:S(2)}, u32[]{:S(2)}) %all-to-all-start) | async-done | bytes 4194336 | tf_op jit(solution)/shard_map/all_to_all | solution.py:246
  69.6 0.0 copy-done.6
  69.6 46.9 %attention.1 = (bf16[32,4,128,128]{3,2,1,0:T(8,128)(2,1)S(1)}, f32[2,128]{1,0:T(2,128)S(1)}) custom-call(s32[1]{0:T(128)S(6)} %copy.14.width_ref, s32[1,2]{1,0:T(1,128)S(1)} %copy-done.6, s32[1,32,3]{2,1,0:T(8,128)S(1)} %copy.13.random_ref, bf16[32,4,128,128]{3,2,1,0:T(8,128)(2,1)} %all-to-all-done.x_ref, f32[2,128]{1,0:T(2,128)S(1)} %constant_dynamic-slice_fusion.1.gain_ref), custom_call_target="tpu_custom_call" | custom-call | tf_op jit(solution)/shard_map/attention/pallas_call | solution.py:181
  116.5 0.0 copy-start.1
  116.5 2.0 copy-done.1
  118.5 7.2 %all-to-all-start.1 = ((bf16[32,4,128,128]{3,2,1,0:T(8,128)(2,1)}), bf16[32,4,128,128]{3,2,1,0:T(8,128)(2,1)}, u32[]{:S(2)}, u32[]{:S(2)}) async-start(bf16[32,4,128,128]{3,2,1,0:T(8,128)(2,1)} %copy-done.1), calls=%async_computation.1 | async-start | bytes 8388608 | tf_op jit(solution)/shard_map/all_to_all | solution.py:246
  125.6 17.9 %psum.7 = f32[2,128]{1,0:T(2,128)S(1)} all-reduce(f32[2,128]{1,0:T(2,128)S(1)} %get-tuple-element.16), channel_id=1, replica_groups=mesh['dp'=8,'ctx'=32] {'dp'}, use_global_device_ids=true, to_apply=%region_0.0 | all-reduce | flops 256 | bytes 2048 | tf_op jit(solution)/shard_map/psum | solution.py:255
  143.5 49.3 %all_gather.7 = f32[2,4096]{1,0:T(2,128)S(1)} all-gather(f32[2,128]{1,0:T(2,128)S(1)} %psum.7), channel_id=1, replica_groups=mesh['dp'=8,'ctx'=32] {'ctx'}, dimensions={1}, use_global_device_ids=true | all-gather | bytes 33792 | tf_op jit(solution)/shard_map/all_gather | solution.py:256
  192.8 0.6 constant_dynamic-slice_fusion
  193.4 0.0 all-to-all-done.1.y_ref
  193.4 5.1 %join_heads.1 = (bf16[1,128,4096]{2,1,0:T(8,128)(2,1)}, bf16[1,128,4096]{2,1,0:T(8,128)(2,1)}, bf16[1,128,4096]{2,1,0:T(8,128)(2,1)}, bf16[1,128,4096]{2,1,0:T(8,128)(2,1)}) custom-call(bf16[32,4,128,128]{3,2,1,0:T(8,128)(2,1)} %all-to-all-done.1.y_ref), custom_call_target="tpu_custom_call" | custom-call | tf_op jit(solution)/shard_map/join_heads/pallas_call | solution.py:234
  (1 shorter events, 0.0 us)
Async XLA Ops:
  0.6 1.2 copy-start.2
  1.9 1.2 copy-start.3
  3.1 1.2 copy-start.4
  4.3 1.2 copy-start.5
  6.6 2.0 copy-start
  8.6 8.8 %copy-start.8 = (s32[1,32,3]{1,0,2:T(1,128)S(1)}, s32[1,32,3]{1,0,2:T(1,128)}, u32[]{:S(2)}) copy-start(s32[1,32,3]{1,0,2:T(1,128)} %param.15) | copy-start | bytes 1156
  8.6 9.5 %copy-start.7 = (f32[2,512]{1,0:T(2,128)S(1)}, f32[2,512]{1,0:T(2,128)}, u32[]{:S(2)}) copy-start(f32[2,512]{1,0:T(2,128)} %param.12) | copy-start | bytes 12292
  8.6 61.0 %copy-start.6 = (s32[1,2]{1,0:T(1,128)S(1)}, s32[1,2]{1,0:T(1,128)}, u32[]{:S(2)}) copy-start(s32[1,2]{1,0:T(1,128)} %global_ref.1) | copy-start | bytes 28
  8.6 61.0 %all-to-all-start = ((bf16[32,4,128,128]{3,2,1,0:T(8,128)(2,1)}), bf16[32,4,128,128]{3,2,1,0:T(8,128)(2,1)}, u32[]{:S(2)}, u32[]{:S(2)}) async-start(bf16[32,4,128,128]{3,2,1,0:T(8,128)(2,1)} %copy-done), calls=%async_computation | async-start | bytes 8388608 | tf_op jit(solution)/shard_map/all_to_all | solution.py:246
  116.5 2.0 copy-start.1
  118.5 75.0 %all-to-all-start.1 = ((bf16[32,4,128,128]{3,2,1,0:T(8,128)(2,1)}), bf16[32,4,128,128]{3,2,1,0:T(8,128)(2,1)}, u32[]{:S(2)}, u32[]{:S(2)}) async-start(bf16[32,4,128,128]{3,2,1,0:T(8,128)(2,1)} %copy-done.1), calls=%async_computation.1 | async-start | bytes 8388608 | tf_op jit(solution)/shard_map/all_to_all | solution.py:246

commit v2 on v1

v2 whole, which is shorter than its diff:
```python
import functools
import math

import jax
import jax.numpy as jnp
from jax import lax
from jax.experimental import pallas as pl
from jax.experimental.pallas import tpu as pltpu
from jax.sharding import PartitionSpec as P

HD = 128
BLOCK = 128
SCALE = 1.0 / math.sqrt(HD)
LOG2E = math.log2(math.e)
SCALE_LOG2 = SCALE * LOG2E
PENALTY = 1e30
CHUNK = 8
GROUP_A = 5
GROUP_B = 5
PARTS = 4
TERM_ROWS = 8
MIB = 1024 * 1024
F32 = jnp.float32
BF16 = jnp.bfloat16
HBM = pl.BlockSpec(memory_space=pltpu.HBM)
VMEM = pl.BlockSpec(memory_space=pltpu.VMEM)
SMEM = pl.BlockSpec(memory_space=pltpu.SMEM)
QUERY, KEY, VALUE, D_OUT = range(4)


def in_hbm(*arrays):
    return [pltpu.with_memory_space_constraint(a, pltpu.HBM) for a in arrays]


def dot_nn(a, b):
    return lax.dot_general(a, b, (((1,), (0,)), ((), ())), preferred_element_type=F32)


def dot_nt(a, b):
    return lax.dot_general(a, b, (((1,), (1,)), ((), ())), preferred_element_type=F32)


def dot_tn(a, b):
    return lax.dot_general(a, b, (((0,), (0,)), ((), ())), preferred_element_type=F32)


def slot_of(wide, t):
    return wide[:, t * BLOCK : (t + 1) * BLOCK]


def lane_fold(combine, wide):
    return functools.reduce(combine, [slot_of(wide, t) for t in range(wide.shape[1] // BLOCK)])


def row_sum(a):
    return jnp.sum(a, axis=1, keepdims=True)


def loop(count, body, start, unroll=True):
    return lax.fori_loop(0, count, body, start, unroll=unroll)


def key_slots(i, width_ref, global_ref, random_ref, block_count):
    wide = width_ref[0] >= 1
    ids = [i]
    penalties = [jnp.float32(0.0)]
    candidates = [(i - 1, wide & (i > 0)), (i + 1, wide & (i < block_count - 1))]
    candidates += [(global_ref[0, n], None) for n in range(2)]
    candidates += [(random_ref[0, i, n], None) for n in range(random_ref.shape[2])]
    for block_id, listed in candidates:
        unusable = functools.reduce(jnp.logical_or, [block_id == t for t in ids])
        if listed is not None:
            unusable = unusable | jnp.logical_not(listed)
        ids.append(jnp.where(unusable, i, block_id))
        penalties.append(jnp.where(unusable, jnp.float32(PENALTY), jnp.float32(0.0)))
    return ids, penalties


def sparse_blocks(step, group, global_ref):
    low = jnp.minimum(global_ref[0, 0], global_ref[0, 1])
    high = jnp.maximum(global_ref[0, 0], global_ref[0, 1])
    blocks = []
    for u in range(group):
        n = step * group + u
        i = n + (n >= low).astype(jnp.int32)
        blocks.append(i + (i >= high).astype(jnp.int32))
    return blocks


def load_all(x_hbm, x_ref, sems):
    copies = [pltpu.make_async_copy(x_hbm.at[:, n], x_ref.at[n], sems.at[n]) for n in range(4)]
    for n in (KEY, QUERY, VALUE, D_OUT):
        copies[n].start()
    return copies


def scale_keys(x_ref, ks_ref, gain_k):
    def body(j, carry):
        ks_ref[j] = (x_ref[KEY, j].astype(F32) * gain_k).astype(BF16)
        return carry

    loop(ks_ref.shape[0], body, 0, 8)


def pair(ref, g0, g1):
    return jnp.concatenate([ref[g0], ref[g1]], 0)


def chunk_of(ref, c):
    return ref[pl.ds(c * CHUNK, CHUNK)].reshape(CHUNK * BLOCK, HD)


def forward_kernel(
    width_ref, global_ref, random_ref, x_hbm, gain_ref, y_hbm, lse_hbm,
    x_ref, ks_ref, p_ref, dv_ref, y_ref, lse_ref, in_sems, out_sems, lse_sem,
):
    copies = load_all(x_hbm, x_ref, in_sems)
    block_count = ks_ref.shape[0]
    chunks = block_count // CHUNK
    gain_q = gain_ref[0:1, :]
    g0 = global_ref[0, 0]
    g1 = global_ref[0, 1]
    k_raw, v_ref, q_ref, d_ref = (x_ref.at[n] for n in (KEY, VALUE, QUERY, D_OUT))
    copies[KEY].wait()
    scale_keys(x_ref, ks_ref, gain_ref[1:2, :])
    copies[QUERY].wait()

    q_scaled = (pair(q_ref, g0, g1).astype(F32) * gain_q).astype(BF16)
    rows = 2 * BLOCK

    def full_scores(c, top):
        scores = dot_nt(q_scaled, chunk_of(ks_ref, c))
        p_ref[c] = scores
        return jnp.maximum(top, lane_fold(jnp.maximum, scores))

    top = loop(chunks, full_scores, jnp.full((rows, BLOCK), -3e38, F32))
    top = jnp.max(top, axis=1, keepdims=True) * SCALE_LOG2

    def full_exp(c, total):
        e = jnp.exp2(p_ref[c] * SCALE_LOG2 - top)
        p_ref[c] = e
        return total + lane_fold(jnp.add, e)

    total = row_sum(loop(chunks, full_exp, jnp.zeros((rows, BLOCK), F32)))
    inverse = 1.0 / total
    lse = jnp.broadcast_to(top + jnp.log(total) * LOG2E, (rows, BLOCK))
    lse_ref[g0] = lse[:BLOCK]
    lse_ref[g1] = lse[BLOCK:]
    copies[VALUE].wait()
    copies[D_OUT].wait()
    d_out = pair(d_ref, g0, g1)

    def full_out(c, acc):
        p_b = (p_ref[c] * inverse).astype(BF16)
        dv_t = dot_tn(d_out, p_b)
        for n in range(CHUNK):
            dv_ref[c * CHUNK + n] = slot_of(dv_t, n)
        return acc + dot_nn(p_b, chunk_of(v_ref, c))

    out = loop(chunks, full_out, jnp.zeros((rows, HD), F32)).astype(BF16)
    y_ref[g0, 0] = out[:BLOCK]
    y_ref[g1, 0] = out[BLOCK:]

    def step(n, carry):
        blocks = sparse_blocks(n, GROUP_A, global_ref)
        us = range(GROUP_A)
        slots = [key_slots(i, width_ref, global_ref, random_ref, block_count) for i in blocks]
        k_slots = [jnp.concatenate([ks_ref[t] for t in slots[u][0]], 0) for u in us]
        v_slots = [jnp.concatenate([v_ref[t] for t in slots[u][0]], 0) for u in us]
        q_scaled = [(q_ref[i].astype(F32) * gain_q).astype(BF16) for i in blocks]
        d_out = [d_ref[i] for i in blocks]
        scores = [dot_nt(q_scaled[u], k_slots[u]) for u in us]
        tops = [
            jnp.max(lane_fold(jnp.maximum, scores[u]), axis=1, keepdims=True) * SCALE_LOG2
            for u in us
        ]
        es = [
            [
                jnp.exp2(slot_of(scores[u], t) * SCALE_LOG2 - (tops[u] + penalty))
                for t, penalty in enumerate(slots[u][1])
            ]
            for u in us
        ]
        totals = [row_sum(functools.reduce(jnp.add, es[u])) for u in us]
        inverses = [1.0 / totals[u] for u in us]
        p_b = [jnp.concatenate([(e * inverses[u]).astype(BF16) for e in es[u]], 1) for u in us]
        outs = [dot_nn(p_b[u], v_slots[u]).astype(BF16) for u in us]
        dv_t = [dot_tn(d_out[u], p_b[u]) for u in us]
        for u in us:
            y_ref[blocks[u], 0] = outs[u]
            lse_ref[blocks[u]] = jnp.broadcast_to(tops[u] + jnp.log(totals[u]) * LOG2E, (BLOCK, BLOCK))
        for u in us:
            for t, block_id in enumerate(slots[u][0]):
                dv_ref[block_id] += slot_of(dv_t[u], t)
        return carry

    lax.fori_loop(0, (block_count - 2) // GROUP_A, step, 0)

    lse_copy = pltpu.make_async_copy(lse_ref, lse_hbm, lse_sem)
    lse_copy.start()

    def finish(j, carry):
        y_ref[j, 1] = dv_ref[j].T.astype(BF16)
        return carry

    out_copies = []
    for part in range(PARTS):
        size = block_count // PARTS
        lax.fori_loop(part * size, (part + 1) * size, finish, 0, unroll=True)
        rows = pl.ds(part * size, size)
        out_copies.append(pltpu.make_async_copy(y_ref.at[rows], y_hbm.at[rows], out_sems.at[part]))
        out_copies[-1].start()
    for copy in out_copies:
        copy.wait()
    lse_copy.wait()


def backward_kernel(
    width_ref, global_ref, random_ref, x_hbm, gain_ref, lse_hbm, out_hbm, y_hbm, terms_ref,
    x_ref, ks_ref, lse_ref, out_ref, dk_ref, y_ref, tq_ref, in_sems, out_sems, lse_sem, o_sem,
):
    copies = load_all(x_hbm, x_ref, in_sems)
    lse_copy = pltpu.make_async_copy(lse_hbm, lse_ref, lse_sem)
    lse_copy.start()
    out_copy = pltpu.make_async_copy(out_hbm.at[:, 0], out_ref, o_sem)
    out_copy.start()
    block_count = ks_ref.shape[0]
    chunks = block_count // CHUNK
    gain_q = gain_ref[0:1, :]
    gain_k = gain_ref[1:2, :]
    g0 = global_ref[0, 0]
    g1 = global_ref[0, 1]
    k_raw, v_ref, q_ref, d_ref = (x_ref.at[n] for n in (KEY, VALUE, QUERY, D_OUT))
    copies[KEY].wait()
    scale_keys(x_ref, ks_ref, gain_k)
    copies[QUERY].wait()
    q_raw = pair(q_ref, g0, g1).astype(F32)
    q_scaled = (q_raw * gain_q).astype(BF16)
    lse_copy.wait()
    lse = jnp.concatenate([pair(lse_ref, g0, g1)] * CHUNK, 1)
    copies[VALUE].wait()
    copies[D_OUT].wait()
    out_copy.wait()
    d_out = pair(d_ref, g0, g1)
    row_dot = row_sum(d_out.astype(F32) * pair(out_ref, g0, g1).astype(F32))

    def full_back(c, acc):
        keys = chunk_of(ks_ref, c)
        p = jnp.exp2(dot_nt(q_scaled, keys) * SCALE_LOG2 - lse)
        ds = (p * (dot_nt(d_out, chunk_of(v_ref, c)) - row_dot)).astype(BF16)
        dk_t = dot_tn(q_scaled, ds)
        for n in range(CHUNK):
            dk_ref[c * CHUNK + n] = slot_of(dk_t, n)
        return acc + dot_nn(ds, keys)

    dq = loop(chunks, full_back, jnp.zeros((2 * BLOCK, HD), F32)) * SCALE
    dq_b = (dq * gain_q).astype(BF16)
    y_ref[g0, 0] = dq_b[:BLOCK]
    y_ref[g1, 0] = dq_b[BLOCK:]
    terms = dq * q_raw
    tq_ref[...] = terms[:BLOCK] + terms[BLOCK:]

    def step(n, carry):
        blocks = sparse_blocks(n, GROUP_B, global_ref)
        us = range(GROUP_B)
        slots = [key_slots(i, width_ref, global_ref, random_ref, block_count) for i in blocks]
        k_slots = [jnp.concatenate([ks_ref[t] for t in slots[u][0]], 0) for u in us]
        v_slots = [jnp.concatenate([v_ref[t] for t in slots[u][0]], 0) for u in us]
        q_raw = [q_ref[i].astype(F32) for i in blocks]
        q_scaled = [(q * gain_q).astype(BF16) for q in q_raw]
        d_out = [d_ref[i] for i in blocks]
        scores = [dot_nt(q_scaled[u], k_slots[u]) for u in us]
        dps = [dot_nt(d_out[u], v_slots[u]) for u in us]
        row_dots = [
            row_sum(d_out[u].astype(F32) * out_ref[blocks[u]].astype(F32)) for u in us
        ]
        ds = []
        for u in us:
            lse = lse_ref[blocks[u]]
            parts = []
            for t, penalty in enumerate(slots[u][1]):
                p = jnp.exp2(slot_of(scores[u], t) * SCALE_LOG2 - (lse + penalty))
                parts.append((p * (slot_of(dps[u], t) - row_dots[u])).astype(BF16))
            ds.append(jnp.concatenate(parts, 1))
        dqs = [dot_nn(ds[u], k_slots[u]) * SCALE for u in us]
        dk_t = [dot_tn(q_scaled[u], ds[u]) for u in us]
        for u in us:
            y_ref[blocks[u], 0] = (dqs[u] * gain_q).astype(BF16)
        tq_ref[...] += functools.reduce(jnp.add, [dqs[u] * q_raw[u] for u in us])
        for u in us:
            for t, block_id in enumerate(slots[u][0]):
                dk_ref[block_id] += slot_of(dk_t[u], t)
        return carry

    lax.fori_loop(0, (block_count - 2) // GROUP_B, step, 0)

    def finish(j, acc):
        dk = dk_ref[j].T * SCALE
        y_ref[j, 1] = (dk * gain_k).astype(BF16)
        return acc + dk * k_raw[j].astype(F32)

    tk = jnp.zeros((BLOCK, HD), F32)
    size = block_count // PARTS
    out_copies = []
    for part in range(PARTS):
        tk = lax.fori_loop(part * size, (part + 1) * size, finish, tk, unroll=True)
        for n in range(2):
            src = y_ref.at[pl.ds(part * size, size), n]
            dst = y_hbm.at[pl.ds(part * size, size), pl.ds(n * BLOCK, BLOCK)]
            out_copies.append(pltpu.make_async_copy(src, dst, out_sems.at[part, n]))
            out_copies[-1].start()
    terms_ref[0:1, :] = jnp.sum(tq_ref[...], axis=0, keepdims=True)
    terms_ref[1:2, :] = jnp.sum(tk, axis=0, keepdims=True)
    for copy in out_copies:
        copy.wait()


def forward(widths, global_ids, random_ids, x, gains):
    blocks = x.shape[0]
    return pl.pallas_call(
        forward_kernel,
        out_shape=(
            pltpu.HBM((blocks, 2, BLOCK, HD), BF16),
            pltpu.HBM((blocks, BLOCK, BLOCK), F32),
        ),
        in_specs=[SMEM, SMEM, SMEM, HBM, VMEM],
        out_specs=(HBM, HBM),
        scratch_shapes=[
            pltpu.VMEM((4, blocks, BLOCK, HD), BF16),
            pltpu.VMEM((blocks, BLOCK, HD), BF16),
            pltpu.VMEM((blocks // CHUNK, 2 * BLOCK, CHUNK * BLOCK), F32),
            pltpu.VMEM((blocks, HD, BLOCK), F32),
            pltpu.VMEM((blocks, 2, BLOCK, HD), BF16),
            pltpu.VMEM((blocks, BLOCK, BLOCK), F32),
            pltpu.SemaphoreType.DMA((4,)),
            pltpu.SemaphoreType.DMA((PARTS,)),
            pltpu.SemaphoreType.DMA,
        ],
        compiler_params=pltpu.CompilerParams(vmem_limit_bytes=36 * MIB),
        name="attention_forward",
    )(widths, global_ids, random_ids, *in_hbm(x), gains)


def backward(widths, global_ids, random_ids, x, gains, lse, y):
    blocks = x.shape[0]
    return pl.pallas_call(
        backward_kernel,
        out_shape=(
            pltpu.HBM((blocks, 2 * BLOCK + TERM_ROWS, HD), BF16),
            jax.ShapeDtypeStruct((2, HD), F32),
        ),
        in_specs=[SMEM, SMEM, SMEM, HBM, VMEM, HBM, HBM],
        out_specs=(HBM, VMEM),
        scratch_shapes=[
            pltpu.VMEM((4, blocks, BLOCK, HD), BF16),
            pltpu.VMEM((blocks, BLOCK, HD), BF16),
            pltpu.VMEM((blocks, BLOCK, BLOCK), F32),
            pltpu.VMEM((blocks, BLOCK, HD), BF16),
            pltpu.VMEM((blocks, HD, BLOCK), F32),
            pltpu.VMEM((blocks, 2, BLOCK, HD), BF16),
            pltpu.VMEM((BLOCK, HD), F32),
            pltpu.SemaphoreType.DMA((4,)),
            pltpu.SemaphoreType.DMA((PARTS, 2)),
            pltpu.SemaphoreType.DMA,
            pltpu.SemaphoreType.DMA,
        ],
        compiler_params=pltpu.CompilerParams(vmem_limit_bytes=36 * MIB),
        name="attention_backward",
    )(widths, global_ids, random_ids, *in_hbm(x), gains, *in_hbm(lse, y))


def put_terms_kernel(y_in, total_ref, y_out, rows_ref, sem):
    total = total_ref[...]
    high = total.astype(BF16)
    low = (total - high.astype(F32)).astype(BF16)
    rows = jnp.concatenate([high, low, jnp.zeros((TERM_ROWS - 4, HD), BF16)], 0)
    rows_ref[...] = jnp.broadcast_to(rows[None], rows_ref.shape)
    copy = pltpu.make_async_copy(rows_ref, y_out.at[:, pl.ds(2 * BLOCK, TERM_ROWS)], sem)
    copy.start()
    copy.wait()


def put_terms(y, total):
    return pl.pallas_call(
        put_terms_kernel,
        out_shape=pltpu.HBM(y.shape, y.dtype),
        in_specs=[HBM, VMEM],
        out_specs=HBM,
        scratch_shapes=[
            pltpu.VMEM((y.shape[0], TERM_ROWS, HD), BF16),
            pltpu.SemaphoreType.DMA,
        ],
        input_output_aliases={0: 0},
        name="put_terms",
    )(*in_hbm(y), total)


def split_kernel(q_hbm, k_hbm, v_hbm, d_hbm, x_hbm, in_ref, x_ref, in_sems, out_sems):
    sources = (q_hbm, k_hbm, v_hbm, d_hbm)
    heads = x_ref.shape[0] // PARTS
    width = heads * HD

    def fetch(c, n):
        src = sources[n].at[0, :, pl.ds(c * width, width)]
        return pltpu.make_async_copy(src, in_ref.at[c, n], in_sems.at[c, n])

    def send(c):
        part = pl.ds(c * heads, heads)
        return pltpu.make_async_copy(x_ref.at[part], x_hbm.at[part], out_sems.at[c])

    for c in range(PARTS):
        for n in range(4):
            fetch(c, n).start()
    for c in range(PARTS):
        for n in range(4):
            fetch(c, n).wait()
            for h in range(heads):
                x_ref[c * heads + h, n] = in_ref[c, n, :, h * HD : (h + 1) * HD]
        send(c).start()
    for c in range(PARTS):
        send(c).wait()


def split_heads(arrays):
    _, tokens, channels = arrays[0].shape
    heads = channels // HD
    return pl.pallas_call(
        split_kernel,
        out_shape=pltpu.HBM((heads, 4, tokens, HD), BF16),
        in_specs=[HBM] * 4,
        out_specs=HBM,
        scratch_shapes=[
            pltpu.VMEM((PARTS, 4, tokens, channels // PARTS), BF16),
            pltpu.VMEM((heads, 4, tokens, HD), BF16),
            pltpu.SemaphoreType.DMA((PARTS, 4)),
            pltpu.SemaphoreType.DMA((PARTS,)),
        ],
        compiler_params=pltpu.CompilerParams(vmem_limit_bytes=16 * MIB),
        name="split_heads",
    )(*in_hbm(*arrays))


def join_pair(z_hbm, targets, in_ref, out_ref, in_sems, out_sems):
    heads = in_ref.shape[0] // PARTS
    width = heads * HD

    def fetch(c):
        part = pl.ds(c * heads, heads)
        src = z_hbm.at[part, pl.ds(0, 2 * BLOCK)]
        return pltpu.make_async_copy(src, in_ref.at[part], in_sems.at[c])

    def send(c, n):
        dst = targets[n].at[0, :, pl.ds(c * width, width)]
        return pltpu.make_async_copy(out_ref.at[c, n], dst, out_sems.at[c, n])

    for c in range(PARTS):
        fetch(c).start()
    for c in range(PARTS):
        fetch(c).wait()
        for n in range(2):
            for h in range(heads):
                rows = in_ref[c * heads + h, n * BLOCK : (n + 1) * BLOCK]
                out_ref[c, n, :, h * HD : (h + 1) * HD] = rows
            send(c, n).start()
    for c in range(PARTS):
        for n in range(2):
            send(c, n).wait()


def join_kernel(z_hbm, a_hbm, b_hbm, in_ref, out_ref, in_sems, out_sems):
    join_pair(z_hbm, (a_hbm, b_hbm), in_ref, out_ref, in_sems, out_sems)


def join_terms_kernel(place_ref, z_ref, a_hbm, b_hbm, gains_ref, out_ref, out_sems):
    targets = (a_hbm, b_hbm)
    heads = z_ref.shape[0] // PARTS
    width = heads * HD
    copies = []
    for c in range(PARTS):
        for n in range(2):
            for h in range(heads):
                rows = z_ref[c * heads + h, n * BLOCK : (n + 1) * BLOCK]
                out_ref[c, n, :, h * HD : (h + 1) * HD] = rows
            dst = targets[n].at[0, :, pl.ds(c * width, width)]
            copies.append(pltpu.make_async_copy(out_ref.at[c, n], dst, out_sems.at[c, n]))
            copies[-1].start()
    own = gains_ref.shape[1] // HD
    for n in range(own):
        rows = z_ref[place_ref[0] * own + n, 2 * BLOCK : 2 * BLOCK + TERM_ROWS].astype(F32)
        gains_ref[:, n * HD : (n + 1) * HD] = rows[0:2] + rows[2:4]
    for copy in copies:
        copy.wait()


def join_scratch(heads, tokens):
    return [
        pltpu.VMEM((heads, 2 * tokens, HD), BF16),
        pltpu.VMEM((PARTS, 2, tokens, heads * HD // PARTS), BF16),
    ], [
        pltpu.SemaphoreType.DMA((PARTS,)),
        pltpu.SemaphoreType.DMA((PARTS, 2)),
    ]


def join_heads(z):
    heads = z.shape[0]
    buffers, sems = join_scratch(heads, BLOCK)
    return pl.pallas_call(
        join_kernel,
        out_shape=(pltpu.HBM((1, BLOCK, heads * HD), BF16),) * 2,
        in_specs=[HBM],
        out_specs=(HBM,) * 2,
        scratch_shapes=buffers + sems,
        compiler_params=pltpu.CompilerParams(vmem_limit_bytes=16 * MIB),
        name="join_heads",
    )(*in_hbm(z))


def join_heads_terms(place, z, own):
    heads = z.shape[0]
    buffers, sems = join_scratch(heads, BLOCK)
    return pl.pallas_call(
        join_terms_kernel,
        out_shape=(pltpu.HBM((1, BLOCK, heads * HD), BF16),) * 2
        + (jax.ShapeDtypeStruct((2, own * HD), F32),),
        in_specs=[SMEM, VMEM],
        out_specs=(HBM, HBM, VMEM),
        scratch_shapes=buffers[1:] + sems[1:],
        compiler_params=pltpu.CompilerParams(vmem_limit_bytes=16 * MIB),
        name="join_heads_terms",
    )(place, z)


def exchange(x):
    return lax.all_to_all(x, "ctx", split_axis=0, concat_axis=0, tiled=True)


def sum_over_sequences(terms):
    count = lax.axis_size("dp")
    stride = 1
    while stride < count:
        pairs = [(n, n ^ stride) for n in range(count)]
        terms = terms + lax.ppermute(terms, "dp", pairs)
        stride *= 2
    return terms


def on_device(queries, keys, values, d_out, gains, window_widths, global_blocks, random_blocks):
    x = exchange(split_heads((queries, keys, values, d_out)))
    all_gains = lax.all_gather(gains, "dp", axis=1, tiled=True)
    own_gains = lax.dynamic_slice_in_dim(all_gains, lax.axis_index("ctx") * HD, HD, 1)
    tables = (window_widths, global_blocks, random_blocks)
    out_dv, lse = forward(*tables, x, own_gains)
    back_out_dv = exchange(out_dv.reshape(-1, 2 * BLOCK, HD))
    dq_dk, terms = backward(*tables, x, own_gains, lse, out_dv)
    dq_dk = put_terms(dq_dk, sum_over_sequences(terms))
    out, d_values = join_heads(back_out_dv)
    place = lax.axis_index("dp").reshape(1)
    d_queries, d_keys, d_gains = join_heads_terms(place, exchange(dq_dk), gains.shape[1] // HD)
    return (out, d_queries, d_keys, d_values, d_gains)


def solution(mesh):
    tokens = P("dp", "ctx", None)
    return jax.shard_map(
        on_device,
        mesh=mesh,
        in_specs=(
            tokens, tokens, tokens, tokens,
            P(None, "dp"), P("ctx"), P("dp", None), P("dp", None, None),
        ),
        out_specs=(tokens, tokens, tokens, tokens, P(None, "dp")),
        check_vma=False,
    )
```

time: 199 us -> 168 us (0.84)
  blocking collectives: 91.5 us -> 24.3 us
  waiting for transfers between devices: 27.2 us -> 57.1 us
  starting transfers between devices: 15.9 us -> 36.9 us
  local copies, waits for them, and re-layouts: 9.5 us -> 1.43 us
  Pallas kernels: 53.1 us -> 45.7 us
    all_gather x1 -> x0, blocking collectives: 49.3 us -> none  [on_device(): columns = lax.all_gather(head_terms, 'ctx', axis=1, tiled=True)]
    all_to_all x2 -> x3, waiting for transfers between devices: 27.2 us -> 53.7 us  [exchange(): return lax.all_to_all(x, 'ctx', split_axis=0, concat_axis=0, tiled=True)]
    psum x1 -> x0, blocking collectives: 17.9 us -> none  [on_device(): head_terms = lax.psum(terms, 'dp')]
    ppermute x0 -> x3, starting transfers between devices: none -> 11 us  [sum_over_sequences(): terms = terms + lax.ppermute(terms, 'dp', pairs)]
    all_to_all x2 -> x3, starting transfers between devices: 15.9 us -> 25.9 us  [exchange(): return lax.all_to_all(x, 'ctx', split_axis=0, concat_axis=0, tiled=True)]
    unnamed x19 -> x9, local copies, waits for them, and re-layouts: 8.9 us -> 1.43 us
    pallas_call x3 -> x6, Pallas kernels: 53.1 us -> 45.7 us  [the longest x1 18.3 us: backward(): pl.pallas_call(backward_kernel, out_shape=(pltpu.HBM((blocks, 2 * BLOCK +...]
    ppermute x0 -> x3, waiting for transfers between devices: none -> 3.46 us  [sum_over_sequences(): terms = terms + lax.ppermute(terms, 'dp', pairs)]
  transfers between devices with their start and end apart: 2 -> 6, of which waited for: 1 -> 5; matrix products, arithmetic and copies ran while one was open for 0% -> 0% of each run, Pallas kernels for 0% -> 13%
where the time goes in v2:
time: 168 us
  waiting for transfers between devices  57.1 us (34%)
  Pallas kernels  45.7 us (27%)
  starting transfers between devices  36.9 us (22%)
  blocking collectives  24.3 us (14%)
    all_to_all x3, waiting for transfers between devices, exchange(): return lax.all_to_all(x, 'ctx', split_axis=0, concat_axis=0, tiled=True)  53.7 us
    all_to_all x3, starting transfers between devices, exchange(): return lax.all_to_all(x, 'ctx', split_axis=0, concat_axis=0, tiled=True)  25.9 us
    all_gather x1, blocking collectives, on_device(): all_gains = lax.all_gather(gains, 'dp', axis=1, tiled=True)  24.3 us
    pallas_call x1, Pallas kernels, backward(): pl.pallas_call(backward_kernel, out_shape=(pltpu.HBM((blocks, 2 * BLOCK +...  18.3 us
    pallas_call x1, Pallas kernels, forward(): pl.pallas_call(forward_kernel, out_shape=(pltpu.HBM((blocks, 2, BLOCK, HD...  18.1 us
    ppermute x3, starting transfers between devices, sum_over_sequences(): terms = terms + lax.ppermute(terms, 'dp', pairs)  11 us
    ppermute x3, waiting for transfers between devices, sum_over_sequences(): terms = terms + lax.ppermute(terms, 'dp', pairs)  3.46 us
    pallas_call x1, Pallas kernels, split_heads(): pl.pallas_call(split_kernel, out_shape=pltpu.HBM((heads, 4, tokens, HD),...  3.46 us
  transfers between devices with their start and end apart: 6, of which 5 were waited for; matrix products, arithmetic and copies ran while one was open for 0% of the time, Pallas kernels for 13%

profile of v2, /device:TPU:1, one launch (start us, length us, event | category | flops | bytes accessed | tf_op | source)
XLA Modules:
  0.0 167.5 jit_solution(20128236361480366)
XLA Ops:
  0.6 3.5 %split_heads.1 = bf16[32,4,128,128]{3,2,1,0:T(8,128)(2,1)} custom-call(bf16[1,128,4096]{2,1,0:T(8,128)(2,1)} %q_hbm.1, bf16[1,128,4096]{2,1,0:T(8,128)(2,1)} %k_hbm.1, bf16[1,128,4096]{2,1,0:T(8,128)(2,1)} %v_hbm.1, bf16[1,128,4096]{2,1,0:T(8,128)(2,1)} %d_hbm.1), custom_call_target="tpu_custom_call" | custom-call | tf_op jit(solution)/shard_map/split_heads/pallas_call | solution.py:427
  4.1 0.0 copy-start.3
  4.1 0.0 copy-start.2
  4.1 0.0 copy-start
  4.1 8.8 %all-to-all-start = ((bf16[32,4,128,128]{3,2,1,0:T(8,128)(2,1)}), bf16[32,4,128,128]{3,2,1,0:T(8,128)(2,1)}, u32[]{:S(2)}, u32[]{:S(2)}) async-start(bf16[32,4,128,128]{3,2,1,0:T(8,128)(2,1)} %split_heads.1), calls=%async_computation | async-start | bytes 8388608 | tf_op jit(solution)/shard_map/all_to_all | solution.py:535
  13.6 0.0 copy-done.3
  13.6 0.1 copy.14.random_ref
  13.7 0.0 copy-done.2
  13.7 24.3 %all_gather.3 = f32[2,4096]{1,0:T(2,128)S(1)} all-gather(f32[2,512]{1,0:T(2,128)S(1)} %copy-done.2), channel_id=1, replica_groups=mesh['dp'=8,'ctx'=32] {'dp'}, dimensions={1}, use_global_device_ids=true | all-gather | bytes 36864 | tf_op jit(solution)/shard_map/all_gather | solution.py:550
  38.0 27.2 %all-to-all-done.x_hbm = bf16[32,4,128,128]{3,2,1,0:T(8,128)(2,1)} async-done(((bf16[32,4,128,128]{3,2,1,0:T(8,128)(2,1)}), bf16[32,4,128,128]{3,2,1,0:T(8,128)(2,1)}, u32[]{:S(2)}, u32[]{:S(2)}) %all-to-all-start) | async-done | bytes 4194336 | tf_op jit(solution)/shard_map/all_to_all | solution.py:535
  65.1 0.0 copy-done
  65.2 18.1 %attention_forward.1 = (bf16[32,2,128,128]{3,2,1,0:T(8,128)(2,1)}, f32[32,128,128]{2,1,0:T(8,128)}) custom-call(s32[1]{0:T(128)S(6)} %copy.17.width_ref, s32[1,2]{1,0:T(1,128)S(1)} %copy-done, s32[1,32,3]{2,1,0:T(8,128)S(1)} %copy.14.random_ref, bf16[32,4,128,128]{3,2,1,0:T(8,128)(2,1)} %all-to-all-done.x_hbm, f32[2,128]{1,0:T(2,128)S(1)} %constant_dynamic-slice_fusion.gain_ref), custom_call_target="tpu_custom_call" | custom-call | tf_op jit(solution)/shard_map/attention_forward/pallas_call | solution.py:320
  83.2 7.1 %all-to-all-start.1 = ((bf16[32,256,128]{2,1,0:T(8,128)(2,1)}), bf16[32,256,128]{2,1,0:T(8,128)(2,1)S(1)}, u32[]{:S(2)}, u32[]{:S(2)}) async-start(bf16[32,256,128]{2,1,0:T(8,128)(2,1)} %bitcast.2), calls=%async_computation.1 | async-start | bytes 4194304 | tf_op jit(solution)/shard_map/all_to_all | solution.py:535
  90.4 18.3 %attention_backward.1 = (bf16[32,264,128]{2,1,0:T(8,128)(2,1)}, f32[2,128]{1,0:T(2,128)S(1)}) custom-call(s32[1]{0:T(128)S(6)} %copy.17.width_ref, s32[1,2]{1,0:T(1,128)S(1)} %copy-done, s32[1,32,3]{2,1,0:T(8,128)S(1)} %copy.14.random_ref, bf16[32,4,128,128]{3,2,1,0:T(8,128)(2,1)} %all-to-all-done.x_hbm, f32[2,128]{1,0:T(2,128)S(1)} %constant_dynamic-slice_fusion.gain_ref, ...), custom_call_target="tpu_custom_call" | custom-call | tf_op jit(solution)/shard_map/attention_backward/pallas_call | solution.py:346
  108.7 1.9 %collective-permute-start = (f32[2,128]{1,0:T(2,128)S(1)}, f32[2,128]{1,0:T(2,128)S(1)}, u32[]{:S(2)}, u32[]{:S(2)}) collective-permute-start(f32[2,128]{1,0:T(2,128)S(1)} %get-tuple-element.18), channel_id=1, source_target_pairs={{0,32},{32,0},{64,96},{96,64},{128,160},{160,128},{192,224},{224,1... | collective-permute-start | bytes 3080 | tf_op jit(solution)/shard_map/ppermute | solution.py:543
  110.6 1.3 collective-permute-done
  111.8 3.0 %collective-permute-start.1 = (f32[2,128]{1,0:T(2,128)S(1)}, f32[2,128]{1,0:T(2,128)S(1)}, u32[]{:S(2)}, u32[]{:S(2)}) collective-permute-start(f32[2,128]{1,0:T(2,128)S(1)} %add.13), channel_id=1, source_target_pairs={{0,64},{32,96},{64,0},{96,32},{128,192},{160,224},{192,128},{224,1... | collective-permute-start | bytes 3080 | tf_op jit(solution)/shard_map/ppermute | solution.py:543
  114.8 1.3 collective-permute-done.1
  116.1 6.1 %collective-permute-start.2 = (f32[2,128]{1,0:T(2,128)S(1)}, f32[2,128]{1,0:T(2,128)S(1)}, u32[]{:S(2)}, u32[]{:S(2)}) collective-permute-start(f32[2,128]{1,0:T(2,128)S(1)} %add.14), channel_id=1, source_target_pairs={{0,128},{32,160},{64,192},{96,224},{128,0},{160,32},{192,64},{224,... | collective-permute-start | bytes 3080 | tf_op jit(solution)/shard_map/ppermute | solution.py:543
  122.2 1.0 collective-permute-done.2
  123.1 0.6 add.15.total_ref
  123.7 1.3 put_terms.1
  125.0 0.0 all-to-all-done.1.z_hbm
  125.0 0.0 copy-start.1
  125.1 1.3 copy-done.1
  126.4 10.0 %all-to-all-start.2 = ((bf16[32,264,128]{2,1,0:T(8,128)(2,1)}), bf16[32,264,128]{2,1,0:T(8,128)(2,1)S(1)}, u32[]{:S(2)}, u32[]{:S(2)}) async-start(bf16[32,264,128]{2,1,0:T(8,128)(2,1)} %put_terms.1), calls=%async_computation.2 | async-start | bytes 4325376 | tf_op jit(solution)/shard_map/all_to_all | solution.py:535
  136.3 2.5 %join_heads.1 = (bf16[1,128,4096]{2,1,0:T(8,128)(2,1)}, bf16[1,128,4096]{2,1,0:T(8,128)(2,1)}) custom-call(bf16[32,256,128]{2,1,0:T(8,128)(2,1)} %copy-done.1), custom_call_target="tpu_custom_call" | custom-call | tf_op jit(solution)/shard_map/join_heads/pallas_call | solution.py:508
  138.9 26.5 %all-to-all-done.2.z_ref = bf16[32,264,128]{2,1,0:T(8,128)(2,1)S(1)} async-done(((bf16[32,264,128]{2,1,0:T(8,128)(2,1)}), bf16[32,264,128]{2,1,0:T(8,128)(2,1)S(1)}, u32[]{:S(2)}, u32[]{:S(2)}) %all-to-all-start.2) | async-done | bytes 2162720 | tf_op jit(solution)/shard_map/all_to_all | solution.py:535
  165.3 2.0 %join_heads_terms.1 = (bf16[1,128,4096]{2,1,0:T(8,128)(2,1)}, bf16[1,128,4096]{2,1,0:T(8,128)(2,1)}, f32[2,512]{1,0:T(2,128)}) custom-call(s32[1]{0:T(128)} %bitcast.1.place_ref, bf16[32,264,128]{2,1,0:T(8,128)(2,1)S(1)} %all-to-all-done.2.z_ref), custom_call_target="tpu_custom_call" | custom-call | tf_op jit(solution)/shard_map/join_heads_terms/pallas_call | solution.py:522
  (3 shorter events, 0.0 us)
Async XLA Ops:
  4.1 9.5 %copy-start.3 = (s32[1,32,3]{1,0,2:T(1,128)S(1)}, s32[1,32,3]{1,0,2:T(1,128)}, u32[]{:S(2)}) copy-start(s32[1,32,3]{1,0,2:T(1,128)} %param.15) | copy-start | bytes 1156
  4.1 9.6 %copy-start.2 = (f32[2,512]{1,0:T(2,128)S(1)}, f32[2,512]{1,0:T(2,128)}, u32[]{:S(2)}) copy-start(f32[2,512]{1,0:T(2,128)} %param.12) | copy-start | bytes 12292
  4.1 61.0 %copy-start = (s32[1,2]{1,0:T(1,128)S(1)}, s32[1,2]{1,0:T(1,128)}, u32[]{:S(2)}) copy-start(s32[1,2]{1,0:T(1,128)} %global_ref.3) | copy-start | bytes 28
  4.1 61.0 %all-to-all-start = ((bf16[32,4,128,128]{3,2,1,0:T(8,128)(2,1)}), bf16[32,4,128,128]{3,2,1,0:T(8,128)(2,1)}, u32[]{:S(2)}, u32[]{:S(2)}) async-start(bf16[32,4,128,128]{3,2,1,0:T(8,128)(2,1)} %split_heads.1), calls=%async_computation | async-start | bytes 8388608 | tf_op jit(solution)/shard_map/all_to_all | solution.py:535
  83.2 41.8 %all-to-all-start.1 = ((bf16[32,256,128]{2,1,0:T(8,128)(2,1)}), bf16[32,256,128]{2,1,0:T(8,128)(2,1)S(1)}, u32[]{:S(2)}, u32[]{:S(2)}) async-start(bf16[32,256,128]{2,1,0:T(8,128)(2,1)} %bitcast.2), calls=%async_computation.1 | async-start | bytes 4194304 | tf_op jit(solution)/shard_map/all_to_all | solution.py:535
  108.7 3.2 %collective-permute-start = (f32[2,128]{1,0:T(2,128)S(1)}, f32[2,128]{1,0:T(2,128)S(1)}, u32[]{:S(2)}, u32[]{:S(2)}) collective-permute-start(f32[2,128]{1,0:T(2,128)S(1)} %get-tuple-element.18), channel_id=1, source_target_pairs={{0,32},{32,0},{64,96},{96,64},{128,160},{160,128},{192,224},{224,1... | collective-permute-start | bytes 3080 | tf_op jit(solution)/shard_map/ppermute | solution.py:543
  111.8 4.2 %collective-permute-start.1 = (f32[2,128]{1,0:T(2,128)S(1)}, f32[2,128]{1,0:T(2,128)S(1)}, u32[]{:S(2)}, u32[]{:S(2)}) collective-permute-start(f32[2,128]{1,0:T(2,128)S(1)} %add.13), channel_id=1, source_target_pairs={{0,64},{32,96},{64,0},{96,32},{128,192},{160,224},{192,128},{224,1... | collective-permute-start | bytes 3080 | tf_op jit(solution)/shard_map/ppermute | solution.py:543
  116.1 7.1 %collective-permute-start.2 = (f32[2,128]{1,0:T(2,128)S(1)}, f32[2,128]{1,0:T(2,128)S(1)}, u32[]{:S(2)}, u32[]{:S(2)}) collective-permute-start(f32[2,128]{1,0:T(2,128)S(1)} %add.14), channel_id=1, source_target_pairs={{0,128},{32,160},{64,192},{96,224},{128,0},{160,32},{192,64},{224,... | collective-permute-start | bytes 3080 | tf_op jit(solution)/shard_map/ppermute | solution.py:543
  125.0 1.3 copy-start.1
  126.4 39.0 %all-to-all-start.2 = ((bf16[32,264,128]{2,1,0:T(8,128)(2,1)}), bf16[32,264,128]{2,1,0:T(8,128)(2,1)S(1)}, u32[]{:S(2)}, u32[]{:S(2)}) async-start(bf16[32,264,128]{2,1,0:T(8,128)(2,1)} %put_terms.1), calls=%async_computation.2 | async-start | bytes 4325376 | tf_op jit(solution)/shard_map/all_to_all | solution.py:535

commit v3 on v2

v3 whole, which is shorter than its diff:
```python
import functools
import math

import jax
import jax.numpy as jnp
from jax import lax
from jax.experimental import pallas as pl
from jax.experimental.pallas import tpu as pltpu
from jax.sharding import PartitionSpec as P

HD = 128
BLOCK = 128
SCALE = 1.0 / math.sqrt(HD)
LOG2E = math.log2(math.e)
SCALE_LOG2 = SCALE * LOG2E
PENALTY = 1e30
CHUNK = 8
GROUP = 5
PARTS = 4
TERM_ROWS = 8
MIB = 1024 * 1024
F32 = jnp.float32
BF16 = jnp.bfloat16
HBM = pl.BlockSpec(memory_space=pltpu.HBM)
VMEM = pl.BlockSpec(memory_space=pltpu.VMEM)
SMEM = pl.BlockSpec(memory_space=pltpu.SMEM)
QUERY, KEY, VALUE, D_OUT = range(4)


def in_hbm(*arrays):
    return [pltpu.with_memory_space_constraint(a, pltpu.HBM) for a in arrays]


def dot_nn(a, b):
    return lax.dot_general(a, b, (((1,), (0,)), ((), ())), preferred_element_type=F32)


def dot_nt(a, b):
    return lax.dot_general(a, b, (((1,), (1,)), ((), ())), preferred_element_type=F32)


def dot_tn(a, b):
    return lax.dot_general(a, b, (((0,), (0,)), ((), ())), preferred_element_type=F32)


def slot_of(wide, t):
    return wide[:, t * BLOCK : (t + 1) * BLOCK]


def lane_fold(combine, wide):
    return functools.reduce(combine, [slot_of(wide, t) for t in range(wide.shape[1] // BLOCK)])


def row_sum(a):
    return jnp.sum(a, axis=1, keepdims=True)


def loop(count, body, start, unroll=True):
    return lax.fori_loop(0, count, body, start, unroll=unroll)


def key_slots(i, width_ref, global_ref, random_ref, block_count):
    wide = width_ref[0] >= 1
    ids = [i]
    penalties = [jnp.float32(0.0)]
    candidates = [(i - 1, wide & (i > 0)), (i + 1, wide & (i < block_count - 1))]
    candidates += [(global_ref[0, n], None) for n in range(2)]
    candidates += [(random_ref[0, i, n], None) for n in range(random_ref.shape[2])]
    for block_id, listed in candidates:
        unusable = functools.reduce(jnp.logical_or, [block_id == t for t in ids])
        if listed is not None:
            unusable = unusable | jnp.logical_not(listed)
        ids.append(jnp.where(unusable, i, block_id))
        penalties.append(jnp.where(unusable, jnp.float32(PENALTY), jnp.float32(0.0)))
    return ids, penalties


def sparse_blocks(step, group, global_ref):
    low = jnp.minimum(global_ref[0, 0], global_ref[0, 1])
    high = jnp.maximum(global_ref[0, 0], global_ref[0, 1])
    blocks = []
    for u in range(group):
        n = step * group + u
        i = n + (n >= low).astype(jnp.int32)
        blocks.append(i + (i >= high).astype(jnp.int32))
    return blocks


def load_all(x_hbm, x_ref, sems):
    copies = [pltpu.make_async_copy(x_hbm.at[:, n], x_ref.at[n], sems.at[n]) for n in range(4)]
    for n in (KEY, QUERY, VALUE, D_OUT):
        copies[n].start()
    return copies


def scale_keys(x_ref, ks_ref, gain_k):
    def body(j, carry):
        ks_ref[j] = (x_ref[KEY, j].astype(F32) * gain_k).astype(BF16)
        return carry

    loop(ks_ref.shape[0], body, 0, 8)


def pair(ref, g0, g1):
    return jnp.concatenate([ref[g0], ref[g1]], 0)


def chunk_of(ref, c):
    return ref[pl.ds(c * CHUNK, CHUNK)].reshape(CHUNK * BLOCK, HD)


def main_kernel(
    width_ref, global_ref, random_ref, x_hbm, gain_ref, y_hbm, lse_hbm, terms_ref,
    x_ref, ks_ref, p_ref, dk_ref, y_ref, lse_ref, tq_ref, in_sems, out_sems, lse_sem,
):
    copies = load_all(x_hbm, x_ref, in_sems)
    block_count = ks_ref.shape[0]
    chunks = block_count // CHUNK
    gain_q = gain_ref[0:1, :]
    gain_k = gain_ref[1:2, :]
    g0 = global_ref[0, 0]
    g1 = global_ref[0, 1]
    k_raw, v_ref, q_ref, d_ref = (x_ref.at[n] for n in (KEY, VALUE, QUERY, D_OUT))
    copies[KEY].wait()
    scale_keys(x_ref, ks_ref, gain_k)
    copies[QUERY].wait()

    q_raw = pair(q_ref, g0, g1).astype(F32)
    q_scaled = (q_raw * gain_q).astype(BF16)
    rows = 2 * BLOCK

    def full_scores(c, top):
        scores = dot_nt(q_scaled, chunk_of(ks_ref, c))
        p_ref[c] = scores
        return jnp.maximum(top, lane_fold(jnp.maximum, scores))

    top = loop(chunks, full_scores, jnp.full((rows, BLOCK), -3e38, F32))
    top = jnp.max(top, axis=1, keepdims=True) * SCALE_LOG2

    def full_exp(c, total):
        e = jnp.exp2(p_ref[c] * SCALE_LOG2 - top)
        p_ref[c] = e
        return total + lane_fold(jnp.add, e)

    total = row_sum(loop(chunks, full_exp, jnp.zeros((rows, BLOCK), F32)))
    inverse = 1.0 / total
    lse = jnp.broadcast_to(top + jnp.log(total) * LOG2E, (rows, BLOCK))
    lse_ref[g0] = lse[:BLOCK]
    lse_ref[g1] = lse[BLOCK:]
    copies[VALUE].wait()
    copies[D_OUT].wait()
    d_out = pair(d_ref, g0, g1)

    def full_out(c, acc):
        p = p_ref[c] * inverse
        p_ref[c] = p
        return acc + dot_nn(p.astype(BF16), chunk_of(v_ref, c))

    out = loop(chunks, full_out, jnp.zeros((rows, HD), F32)).astype(BF16)
    y_ref[g0, 0] = out[:BLOCK]
    y_ref[g1, 0] = out[BLOCK:]
    row_dot = row_sum(d_out.astype(F32) * out.astype(F32))

    def full_back(c, acc):
        ds = (p_ref[c] * (dot_nt(d_out, chunk_of(v_ref, c)) - row_dot)).astype(BF16)
        dk_t = dot_tn(q_scaled, ds)
        for n in range(CHUNK):
            dk_ref[c * CHUNK + n] = slot_of(dk_t, n)
        return acc + dot_nn(ds, chunk_of(ks_ref, c))

    dq = loop(chunks, full_back, jnp.zeros((rows, HD), F32)) * SCALE
    dq_b = (dq * gain_q).astype(BF16)
    y_ref[g0, 1] = dq_b[:BLOCK]
    y_ref[g1, 1] = dq_b[BLOCK:]
    terms = dq * q_raw
    tq_ref[...] = terms[:BLOCK] + terms[BLOCK:]

    def step(n, carry):
        blocks = sparse_blocks(n, GROUP, global_ref)
        us = range(GROUP)
        slots = [key_slots(i, width_ref, global_ref, random_ref, block_count) for i in blocks]
        k_slots = [jnp.concatenate([ks_ref[t] for t in slots[u][0]], 0) for u in us]
        v_slots = [jnp.concatenate([v_ref[t] for t in slots[u][0]], 0) for u in us]
        q_raw = [q_ref[i].astype(F32) for i in blocks]
        q_scaled = [(q * gain_q).astype(BF16) for q in q_raw]
        d_out = [d_ref[i] for i in blocks]
        scores = [dot_nt(q_scaled[u], k_slots[u]) for u in us]
        dps = [dot_nt(d_out[u], v_slots[u]) for u in us]
        tops = [
            jnp.max(lane_fold(jnp.maximum, scores[u]), axis=1, keepdims=True) * SCALE_LOG2
            for u in us
        ]
        es = [
            [
                jnp.exp2(slot_of(scores[u], t) * SCALE_LOG2 - (tops[u] + penalty))
                for t, penalty in enumerate(slots[u][1])
            ]
            for u in us
        ]
        totals = [row_sum(functools.reduce(jnp.add, es[u])) for u in us]
        inverses = [1.0 / totals[u] for u in us]
        ps = [[e * inverses[u] for e in es[u]] for u in us]
        p_b = [jnp.concatenate([p.astype(BF16) for p in ps[u]], 1) for u in us]
        outs = [dot_nn(p_b[u], v_slots[u]).astype(BF16) for u in us]
        row_dots = [row_sum(d_out[u].astype(F32) * outs[u].astype(F32)) for u in us]
        ds = [
            jnp.concatenate(
                [
                    (p * (slot_of(dps[u], t) - row_dots[u])).astype(BF16)
                    for t, p in enumerate(ps[u])
                ],
                1,
            )
            for u in us
        ]
        dqs = [dot_nn(ds[u], k_slots[u]) * SCALE for u in us]
        dk_t = [dot_tn(q_scaled[u], ds[u]) for u in us]
        for u in us:
            y_ref[blocks[u], 0] = outs[u]
            y_ref[blocks[u], 1] = (dqs[u] * gain_q).astype(BF16)
            lse_ref[blocks[u]] = jnp.broadcast_to(
                tops[u] + jnp.log(totals[u]) * LOG2E, (BLOCK, BLOCK)
            )
        tq_ref[...] += functools.reduce(jnp.add, [dqs[u] * q_raw[u] for u in us])
        for u in us:
            for t, block_id in enumerate(slots[u][0]):
                dk_ref[block_id] += slot_of(dk_t[u], t)
        return carry

    lax.fori_loop(0, (block_count - 2) // GROUP, step, 0)
    lse_copy = pltpu.make_async_copy(lse_ref, lse_hbm, lse_sem)

    def finish(j, acc):
        dk = dk_ref[j].T * SCALE
        y_ref[j, 2] = (dk * gain_k).astype(BF16)
        return acc + dk * k_raw[j].astype(F32)

    tk = jnp.zeros((BLOCK, HD), F32)
    size = block_count // PARTS
    out_copies = []
    for part in range(PARTS):
        tk = lax.fori_loop(part * size, (part + 1) * size, finish, tk, unroll=True)
        rows = pl.ds(part * size, size)
        out_copies.append(pltpu.make_async_copy(y_ref.at[rows], y_hbm.at[rows], out_sems.at[part]))
        out_copies[-1].start()
    lse_copy.start()
    terms_ref[0:1, :] = jnp.sum(tq_ref[...], axis=0, keepdims=True)
    terms_ref[1:2, :] = jnp.sum(tk, axis=0, keepdims=True)
    for copy in out_copies:
        copy.wait()
    lse_copy.wait()


def values_kernel(
    width_ref, global_ref, random_ref, x_hbm, gain_ref, lse_hbm, y_hbm,
    x_ref, ks_ref, lse_ref, dv_ref, y_ref, in_sems, lse_sem, out_sem,
):
    lse_copy = pltpu.make_async_copy(lse_hbm, lse_ref, lse_sem)
    lse_copy.start()
    copies = [
        pltpu.make_async_copy(x_hbm.at[:, n], x_ref.at[n], in_sems.at[n])
        for n in (KEY, QUERY, D_OUT)
    ]
    for copy in copies:
        copy.start()
    block_count = ks_ref.shape[0]
    chunks = block_count // CHUNK
    gain_q = gain_ref[0:1, :]
    g0 = global_ref[0, 0]
    g1 = global_ref[0, 1]
    q_ref, d_ref = x_ref.at[QUERY], x_ref.at[D_OUT]
    lse_copy.wait()
    for copy in copies:
        copy.wait()
    scale_keys(x_ref, ks_ref, gain_ref[1:2, :])
    q_scaled = (pair(q_ref, g0, g1).astype(F32) * gain_q).astype(BF16)
    lse = jnp.concatenate([pair(lse_ref, g0, g1)] * CHUNK, 1)
    d_out = pair(d_ref, g0, g1)

    def full_values(c, carry):
        scores = dot_nt(q_scaled, chunk_of(ks_ref, c))
        dv_t = dot_tn(d_out, jnp.exp2(scores * SCALE_LOG2 - lse).astype(BF16))
        for n in range(CHUNK):
            dv_ref[c * CHUNK + n] = slot_of(dv_t, n)
        return carry

    loop(chunks, full_values, 0)

    def step(n, carry):
        blocks = sparse_blocks(n, GROUP, global_ref)
        us = range(GROUP)
        slots = [key_slots(i, width_ref, global_ref, random_ref, block_count) for i in blocks]
        k_slots = [jnp.concatenate([ks_ref[t] for t in slots[u][0]], 0) for u in us]
        q_scaled = [(q_ref[i].astype(F32) * gain_q).astype(BF16) for i in blocks]
        scores = [dot_nt(q_scaled[u], k_slots[u]) for u in us]
        dv_t = []
        for u in us:
            lse = lse_ref[blocks[u]]
            p_b = [
                jnp.exp2(slot_of(scores[u], t) * SCALE_LOG2 - (lse + penalty)).astype(BF16)
                for t, penalty in enumerate(slots[u][1])
            ]
            dv_t.append(dot_tn(d_ref[blocks[u]], jnp.concatenate(p_b, 1)))
        for u in us:
            for t, block_id in enumerate(slots[u][0]):
                dv_ref[block_id] += slot_of(dv_t[u], t)
        return carry

    lax.fori_loop(0, (block_count - 2) // GROUP, step, 0)

    def finish(j, carry):
        y_ref[j] = dv_ref[j].T.astype(BF16)
        return carry

    loop(block_count, finish, 0, 8)
    copy = pltpu.make_async_copy(y_ref, y_hbm.at[:, pl.ds(0, BLOCK)], out_sem)
    copy.start()
    copy.wait()


def attend_without_values(widths, global_ids, random_ids, x, gains):
    blocks = x.shape[0]
    return pl.pallas_call(
        main_kernel,
        out_shape=(
            pltpu.HBM((blocks, 3, BLOCK, HD), BF16),
            pltpu.HBM((blocks, BLOCK, BLOCK), F32),
            jax.ShapeDtypeStruct((2, HD), F32),
        ),
        in_specs=[SMEM, SMEM, SMEM, HBM, VMEM],
        out_specs=(HBM, HBM, VMEM),
        scratch_shapes=[
            pltpu.VMEM((4, blocks, BLOCK, HD), BF16),
            pltpu.VMEM((blocks, BLOCK, HD), BF16),
            pltpu.VMEM((blocks // CHUNK, 2 * BLOCK, CHUNK * BLOCK), F32),
            pltpu.VMEM((blocks, HD, BLOCK), F32),
            pltpu.VMEM((blocks, 3, BLOCK, HD), BF16),
            pltpu.VMEM((blocks, BLOCK, BLOCK), F32),
            pltpu.VMEM((BLOCK, HD), F32),
            pltpu.SemaphoreType.DMA((4,)),
            pltpu.SemaphoreType.DMA((PARTS,)),
            pltpu.SemaphoreType.DMA,
        ],
        compiler_params=pltpu.CompilerParams(vmem_limit_bytes=40 * MIB),
        name="attend_without_values",
    )(widths, global_ids, random_ids, *in_hbm(x), gains)


def value_gradients(widths, global_ids, random_ids, x, gains, lse):
    blocks = x.shape[0]
    return pl.pallas_call(
        values_kernel,
        out_shape=pltpu.HBM((blocks, BLOCK + TERM_ROWS, HD), BF16),
        in_specs=[SMEM, SMEM, SMEM, HBM, VMEM, HBM],
        out_specs=HBM,
        scratch_shapes=[
            pltpu.VMEM((4, blocks, BLOCK, HD), BF16),
            pltpu.VMEM((blocks, BLOCK, HD), BF16),
            pltpu.VMEM((blocks, BLOCK, BLOCK), F32),
            pltpu.VMEM((blocks, HD, BLOCK), F32),
            pltpu.VMEM((blocks, BLOCK, HD), BF16),
            pltpu.SemaphoreType.DMA((4,)),
            pltpu.SemaphoreType.DMA,
            pltpu.SemaphoreType.DMA,
        ],
        compiler_params=pltpu.CompilerParams(vmem_limit_bytes=40 * MIB),
        name="value_gradients",
    )(widths, global_ids, random_ids, *in_hbm(x), gains, *in_hbm(lse))


def put_terms_kernel(y_in, total_ref, y_out, rows_ref, sem):
    total = total_ref[...]
    high = total.astype(BF16)
    low = (total - high.astype(F32)).astype(BF16)
    rows = jnp.concatenate([high, low, jnp.zeros((TERM_ROWS - 4, HD), BF16)], 0)
    rows_ref[...] = jnp.broadcast_to(rows[None], rows_ref.shape)
    copy = pltpu.make_async_copy(rows_ref, y_out.at[:, pl.ds(BLOCK, TERM_ROWS)], sem)
    copy.start()
    copy.wait()


def put_terms(y, total):
    return pl.pallas_call(
        put_terms_kernel,
        out_shape=pltpu.HBM(y.shape, y.dtype),
        in_specs=[HBM, VMEM],
        out_specs=HBM,
        scratch_shapes=[
            pltpu.VMEM((y.shape[0], TERM_ROWS, HD), BF16),
            pltpu.SemaphoreType.DMA,
        ],
        input_output_aliases={0: 0},
        name="put_terms",
    )(*in_hbm(y), total)


def split_kernel(q_hbm, k_hbm, v_hbm, d_hbm, x_hbm, in_ref, x_ref, in_sems, out_sems):
    sources = (q_hbm, k_hbm, v_hbm, d_hbm)
    heads = x_ref.shape[0] // PARTS
    width = heads * HD

    def fetch(c, n):
        src = sources[n].at[0, :, pl.ds(c * width, width)]
        return pltpu.make_async_copy(src, in_ref.at[c, n], in_sems.at[c, n])

    def send(c):
        part = pl.ds(c * heads, heads)
        return pltpu.make_async_copy(x_ref.at[part], x_hbm.at[part], out_sems.at[c])

    for c in range(PARTS):
        for n in range(4):
            fetch(c, n).start()
    for c in range(PARTS):
        for n in range(4):
            fetch(c, n).wait()
            for h in range(heads):
                x_ref[c * heads + h, n] = in_ref[c, n, :, h * HD : (h + 1) * HD]
        send(c).start()
    for c in range(PARTS):
        send(c).wait()


def split_heads(arrays):
    _, tokens, channels = arrays[0].shape
    heads = channels // HD
    return pl.pallas_call(
        split_kernel,
        out_shape=pltpu.HBM((heads, 4, tokens, HD), BF16),
        in_specs=[HBM] * 4,
        out_specs=HBM,
        scratch_shapes=[
            pltpu.VMEM((PARTS, 4, tokens, channels // PARTS), BF16),
            pltpu.VMEM((heads, 4, tokens, HD), BF16),
            pltpu.SemaphoreType.DMA((PARTS, 4)),
            pltpu.SemaphoreType.DMA((PARTS,)),
        ],
        compiler_params=pltpu.CompilerParams(vmem_limit_bytes=16 * MIB),
        name="split_heads",
    )(*in_hbm(*arrays))


def join_kernel(z_hbm, a_hbm, b_hbm, c_hbm, in_ref, out_ref, in_sems, out_sems):
    targets = (a_hbm, b_hbm, c_hbm)
    heads = in_ref.shape[0] // PARTS
    width = heads * HD

    def fetch(c):
        part = pl.ds(c * heads, heads)
        return pltpu.make_async_copy(z_hbm.at[part], in_ref.at[part], in_sems.at[c])

    def send(c, n):
        dst = targets[n].at[0, :, pl.ds(c * width, width)]
        return pltpu.make_async_copy(out_ref.at[c, n], dst, out_sems.at[c, n])

    for c in range(PARTS):
        fetch(c).start()
    for c in range(PARTS):
        fetch(c).wait()
        for n in range(3):
            for h in range(heads):
                out_ref[c, n, :, h * HD : (h + 1) * HD] = in_ref[c * heads + h, n]
            send(c, n).start()
    for c in range(PARTS):
        for n in range(3):
            send(c, n).wait()


def join_terms_kernel(place_ref, z_ref, a_hbm, gains_ref, out_ref, out_sems):
    heads = z_ref.shape[0] // PARTS
    width = heads * HD
    copies = []
    for c in range(PARTS):
        for h in range(heads):
            out_ref[c, :, h * HD : (h + 1) * HD] = z_ref[c * heads + h, 0:BLOCK]
        dst = a_hbm.at[0, :, pl.ds(c * width, width)]
        copies.append(pltpu.make_async_copy(out_ref.at[c], dst, out_sems.at[c]))
        copies[-1].start()
    own = gains_ref.shape[1] // HD
    for n in range(own):
        rows = z_ref[place_ref[0] * own + n, BLOCK : BLOCK + TERM_ROWS].astype(F32)
        gains_ref[:, n * HD : (n + 1) * HD] = rows[0:2] + rows[2:4]
    for copy in copies:
        copy.wait()


def join_heads(z):
    heads = z.shape[0]
    return pl.pallas_call(
        join_kernel,
        out_shape=(pltpu.HBM((1, BLOCK, heads * HD), BF16),) * 3,
        in_specs=[HBM],
        out_specs=(HBM,) * 3,
        scratch_shapes=[
            pltpu.VMEM((heads, 3, BLOCK, HD), BF16),
            pltpu.VMEM((PARTS, 3, BLOCK, heads * HD // PARTS), BF16),
            pltpu.SemaphoreType.DMA((PARTS,)),
            pltpu.SemaphoreType.DMA((PARTS, 3)),
        ],
        compiler_params=pltpu.CompilerParams(vmem_limit_bytes=16 * MIB),
        name="join_heads",
    )(*in_hbm(z))


def join_heads_terms(place, z, own):
    heads = z.shape[0]
    return pl.pallas_call(
        join_terms_kernel,
        out_shape=(
            pltpu.HBM((1, BLOCK, heads * HD), BF16),
            jax.ShapeDtypeStruct((2, own * HD), F32),
        ),
        in_specs=[SMEM, VMEM],
        out_specs=(HBM, VMEM),
        scratch_shapes=[
            pltpu.VMEM((PARTS, BLOCK, heads * HD // PARTS), BF16),
            pltpu.SemaphoreType.DMA((PARTS,)),
        ],
        compiler_params=pltpu.CompilerParams(vmem_limit_bytes=16 * MIB),
        name="join_heads_terms",
    )(place, z)


def exchange(x):
    return lax.all_to_all(x, "ctx", split_axis=0, concat_axis=0, tiled=True)


def sum_over_sequences(terms):
    count = lax.axis_size("dp")
    stride = 1
    while stride < count:
        pairs = [(n, n ^ stride) for n in range(count)]
        terms = terms + lax.ppermute(terms, "dp", pairs)
        stride *= 2
    return terms


def on_device(queries, keys, values, d_out, gains, window_widths, global_blocks, random_blocks):
    x = exchange(split_heads((queries, keys, values, d_out)))
    all_gains = lax.all_gather(gains, "dp", axis=1, tiled=True)
    own_gains = lax.dynamic_slice_in_dim(all_gains, lax.axis_index("ctx") * HD, HD, 1)
    tables = (window_widths, global_blocks, random_blocks)
    y, lse, terms = attend_without_values(*tables, x, own_gains)
    returned = exchange(y)
    d_values = value_gradients(*tables, x, own_gains, lse)
    d_values = put_terms(d_values, sum_over_sequences(terms))
    out, d_queries, d_keys = join_heads(returned)
    place = lax.axis_index("dp").reshape(1)
    d_values, d_gains = join_heads_terms(place, exchange(d_values), gains.shape[1] // HD)
    return (out, d_queries, d_keys, d_values, d_gains)


def solution(mesh):
    tokens = P("dp", "ctx", None)
    return jax.shard_map(
        on_device,
        mesh=mesh,
        in_specs=(
            tokens, tokens, tokens, tokens,
            P(None, "dp"), P("ctx"), P("dp", None), P("dp", None, None),
        ),
        out_specs=(tokens, tokens, tokens, tokens, P(None, "dp")),
        check_vma=False,
    )
```

time: 168 us -> 192 us (1.14)
  blocking collectives: 24.3 us -> 52.4 us
  starting transfers between devices: 36.9 us -> 24.4 us
  waiting for transfers between devices: 57.1 us -> 67.4 us
    all_to_all x0 -> x1, blocking collectives: none -> 28.1 us  [exchange(): return lax.all_to_all(x, 'ctx', split_axis=0, concat_axis=0, tiled=True)]
    all_to_all x3 -> x2, starting transfers between devices: 25.9 us -> 13.6 us  [exchange(): return lax.all_to_all(x, 'ctx', split_axis=0, concat_axis=0, tiled=True)]
    all_to_all x3 -> x2, waiting for transfers between devices: 53.7 us -> 65.5 us  [exchange(): return lax.all_to_all(x, 'ctx', split_axis=0, concat_axis=0, tiled=True)]
  transfers between devices with their start and end apart: 6 -> 5, of which waited for: 5 -> 4; matrix products, arithmetic and copies ran while one was open for 0% -> 0% of each run, Pallas kernels for 13% -> 8%
where the time goes in v3:
time: 192 us
  waiting for transfers between devices  67.4 us (35%)
  blocking collectives  52.4 us (27%)
  Pallas kernels  45.3 us (24%)
  starting transfers between devices  24.4 us (13%)
    all_to_all x2, waiting for transfers between devices, exchange(): return lax.all_to_all(x, 'ctx', split_axis=0, concat_axis=0, tiled=True)  65.5 us
    all_to_all x1, blocking collectives, exchange(): return lax.all_to_all(x, 'ctx', split_axis=0, concat_axis=0, tiled=True)  28.1 us
    all_gather x1, blocking collectives, on_device(): all_gains = lax.all_gather(gains, 'dp', axis=1, tiled=True)  24.3 us
    pallas_call x1, Pallas kernels, attend_without_values(): pl.pallas_call(main_kernel, out_shape=(pltpu.HBM((blocks, 3, BLOCK, HD),...  23 us
    all_to_all x2, starting transfers between devices, exchange(): return lax.all_to_all(x, 'ctx', split_axis=0, concat_axis=0, tiled=True)  13.6 us
    pallas_call x1, Pallas kernels, value_gradients(): pl.pallas_call(values_kernel, out_shape=pltpu.HBM((blocks, BLOCK + TERM_R...  12.8 us
    ppermute x3, starting transfers between devices, sum_over_sequences(): terms = terms + lax.ppermute(terms, 'dp', pairs)  10.8 us
  transfers between devices with their start and end apart: 5, of which 4 were waited for; matrix products, arithmetic and copies ran while one was open for 0% of the time, Pallas kernels for 8%

profile of v3, /device:TPU:1, one launch (start us, length us, event | category | flops | bytes accessed | tf_op | source)
XLA Modules:
  0.0 191.6 jit_solution(17604965391113107999)
XLA Ops:
  0.6 3.4 %split_heads.1 = bf16[32,4,128,128]{3,2,1,0:T(8,128)(2,1)} custom-call(bf16[1,128,4096]{2,1,0:T(8,128)(2,1)} %q_hbm.1, bf16[1,128,4096]{2,1,0:T(8,128)(2,1)} %k_hbm.1, bf16[1,128,4096]{2,1,0:T(8,128)(2,1)} %v_hbm.1, bf16[1,128,4096]{2,1,0:T(8,128)(2,1)} %d_hbm.1), custom_call_target="tpu_custom_call" | custom-call | tf_op jit(solution)/shard_map/split_heads/pallas_call | solution.py:426
  4.1 0.0 copy-start.2
  4.1 0.0 copy-start.1
  4.1 0.0 copy-start
  4.1 8.8 %all-to-all-start = ((bf16[32,4,128,128]{3,2,1,0:T(8,128)(2,1)}), bf16[32,4,128,128]{3,2,1,0:T(8,128)(2,1)}, u32[]{:S(2)}, u32[]{:S(2)}) async-start(bf16[32,4,128,128]{3,2,1,0:T(8,128)(2,1)} %split_heads.1), calls=%async_computation | async-start | bytes 8388608 | tf_op jit(solution)/shard_map/all_to_all | solution.py:524
  13.6 0.0 copy-done.2
  13.6 0.1 copy.14.random_ref
  13.7 0.0 copy-done.1
  13.7 24.3 %all_gather.3 = f32[2,4096]{1,0:T(2,128)S(1)} all-gather(f32[2,512]{1,0:T(2,128)S(1)} %copy-done.1), channel_id=1, replica_groups=mesh['dp'=8,'ctx'=32] {'dp'}, dimensions={1}, use_global_device_ids=true | all-gather | bytes 36864 | tf_op jit(solution)/shard_map/all_gather | solution.py:539
  37.9 27.2 %all-to-all-done.x_hbm = bf16[32,4,128,128]{3,2,1,0:T(8,128)(2,1)} async-done(((bf16[32,4,128,128]{3,2,1,0:T(8,128)(2,1)}), bf16[32,4,128,128]{3,2,1,0:T(8,128)(2,1)}, u32[]{:S(2)}, u32[]{:S(2)}) %all-to-all-start) | async-done | bytes 4194336 | tf_op jit(solution)/shard_map/all_to_all | solution.py:524
  65.1 0.0 copy-done
  65.1 23.0 %attend_without_values.1 = (bf16[32,3,128,128]{3,2,1,0:T(8,128)(2,1)}, f32[32,128,128]{2,1,0:T(8,128)}, f32[2,128]{1,0:T(2,128)S(1)}) custom-call(s32[1]{0:T(128)S(6)} %copy.17.width_ref, s32[1,2]{1,0:T(1,128)S(1)} %copy-done, s32[1,32,3]{2,1,0:T(8,128)S(1)} %copy.14.random_ref, bf16[32,4,128,128]{3,2,1,0:T(8,128)(2,1)} %all-to-all-done.x_hbm, ...), custom_call_target="tpu_custom_call" | custom-call | tf_op jit(solution)/shard_map/attend_without_values/pallas_call | solution.py:323
  88.1 1.7 collective-permute-start
  89.9 1.0 collective-permute-done
  90.8 3.0 %collective-permute-start.1 = (f32[2,128]{1,0:T(2,128)S(1)}, f32[2,128]{1,0:T(2,128)S(1)}, u32[]{:S(2)}, u32[]{:S(2)}) collective-permute-start(f32[2,128]{1,0:T(2,128)S(1)} %add.13), channel_id=1, source_target_pairs={{0,64},{32,96},{64,0},{96,32},{128,192},{160,224},{192,128},{224,1... | collective-permute-start | bytes 3080 | tf_op jit(solution)/shard_map/ppermute | solution.py:532
  93.8 1.0 collective-permute-done.1
  94.8 6.1 %collective-permute-start.2 = (f32[2,128]{1,0:T(2,128)S(1)}, f32[2,128]{1,0:T(2,128)S(1)}, u32[]{:S(2)}, u32[]{:S(2)}) collective-permute-start(f32[2,128]{1,0:T(2,128)S(1)} %add.14), channel_id=1, source_target_pairs={{0,128},{32,160},{64,192},{96,224},{128,0},{160,32},{192,64},{224,... | collective-permute-start | bytes 3080 | tf_op jit(solution)/shard_map/ppermute | solution.py:532
  100.9 12.8 %value_gradients.1.y_in = bf16[32,136,128]{2,1,0:T(8,128)(2,1)} custom-call(s32[1]{0:T(128)S(6)} %copy.17.width_ref, s32[1,2]{1,0:T(1,128)S(1)} %copy-done, s32[1,32,3]{2,1,0:T(8,128)S(1)} %copy.14.random_ref, bf16[32,4,128,128]{3,2,1,0:T(8,128)(2,1)} %all-to-all-done.x_hbm, f32[2,128]{1,0:T(2,128)S(1)} %constant_dynamic-slice_fusion.gain_ref, ...), custom_call_target="tpu_custom_call" | custom-call | tf_op jit(solution)/shard_map/value_gradients/pallas_call | solution.py:351
  113.7 0.0 collective-permute-done.2
  113.7 0.6 add.15.total_ref
  114.3 1.3 put_terms.1
  115.7 28.1 %all_to_all.15.z_ref = bf16[32,136,128]{2,1,0:T(8,128)(2,1)S(1)} all-to-all(bf16[32,136,128]{2,1,0:T(8,128)(2,1)} %put_terms.1), channel_id=1, replica_groups=mesh['dp'=8,'ctx'=32] {'ctx'}, dimensions={0} | all-to-all | bytes 2228224 | tf_op jit(solution)/shard_map/all_to_all | solution.py:524
  143.8 4.8 %all-to-all-start.1 = ((bf16[32,3,128,128]{3,2,1,0:T(8,128)(2,1)}), bf16[32,3,128,128]{3,2,1,0:T(8,128)(2,1)}, u32[]{:S(2)}, u32[]{:S(2)}) async-start(bf16[32,3,128,128]{3,2,1,0:T(8,128)(2,1)} %get-tuple-element.13), calls=%async_computation.1 | async-start | bytes 6291456 | tf_op jit(solution)/shard_map/all_to_all | solution.py:524
  148.6 1.7 join_heads_terms.1
  150.2 38.3 %all-to-all-done.1.z_hbm = bf16[32,3,128,128]{3,2,1,0:T(8,128)(2,1)} async-done(((bf16[32,3,128,128]{3,2,1,0:T(8,128)(2,1)}), bf16[32,3,128,128]{3,2,1,0:T(8,128)(2,1)}, u32[]{:S(2)}, u32[]{:S(2)}) %all-to-all-start.1) | async-done | bytes 3145760 | tf_op jit(solution)/shard_map/all_to_all | solution.py:524
  188.5 3.0 %join_heads.1 = (bf16[1,128,4096]{2,1,0:T(8,128)(2,1)}, bf16[1,128,4096]{2,1,0:T(8,128)(2,1)}, bf16[1,128,4096]{2,1,0:T(8,128)(2,1)}) custom-call(bf16[32,3,128,128]{3,2,1,0:T(8,128)(2,1)} %all-to-all-done.1.z_hbm), custom_call_target="tpu_custom_call" | custom-call | tf_op jit(solution)/shard_map/join_heads/pallas_call | solution.py:488
  (3 shorter events, 0.0 us)
Async XLA Ops:
  4.1 9.5 %copy-start.2 = (s32[1,32,3]{1,0,2:T(1,128)S(1)}, s32[1,32,3]{1,0,2:T(1,128)}, u32[]{:S(2)}) copy-start(s32[1,32,3]{1,0,2:T(1,128)} %param.15) | copy-start | bytes 1156
  4.1 9.6 %copy-start.1 = (f32[2,512]{1,0:T(2,128)S(1)}, f32[2,512]{1,0:T(2,128)}, u32[]{:S(2)}) copy-start(f32[2,512]{1,0:T(2,128)} %param.12) | copy-start | bytes 12292
  4.1 61.0 %copy-start = (s32[1,2]{1,0:T(1,128)S(1)}, s32[1,2]{1,0:T(1,128)}, u32[]{:S(2)}) copy-start(s32[1,2]{1,0:T(1,128)} %global_ref.3) | copy-start | bytes 28
  4.1 61.0 %all-to-all-start = ((bf16[32,4,128,128]{3,2,1,0:T(8,128)(2,1)}), bf16[32,4,128,128]{3,2,1,0:T(8,128)(2,1)}, u32[]{:S(2)}, u32[]{:S(2)}) async-start(bf16[32,4,128,128]{3,2,1,0:T(8,128)(2,1)} %split_heads.1), calls=%async_computation | async-start | bytes 8388608 | tf_op jit(solution)/shard_map/all_to_all | solution.py:524
  88.1 2.7 %collective-permute-start = (f32[2,128]{1,0:T(2,128)S(1)}, f32[2,128]{1,0:T(2,128)S(1)}, u32[]{:S(2)}, u32[]{:S(2)}) collective-permute-start(f32[2,128]{1,0:T(2,128)S(1)} %get-tuple-element.18), channel_id=1, source_target_pairs={{0,32},{32,0},{64,96},{96,64},{128,160},{160,128},{192,224},{224,1... | collective-permute-start | bytes 3080 | tf_op jit(solution)/shard_map/ppermute | solution.py:532
  90.8 3.9 %collective-permute-start.1 = (f32[2,128]{1,0:T(2,128)S(1)}, f32[2,128]{1,0:T(2,128)S(1)}, u32[]{:S(2)}, u32[]{:S(2)}) collective-permute-start(f32[2,128]{1,0:T(2,128)S(1)} %add.13), channel_id=1, source_target_pairs={{0,64},{32,96},{64,0},{96,32},{128,192},{160,224},{192,128},{224,1... | collective-permute-start | bytes 3080 | tf_op jit(solution)/shard_map/ppermute | solution.py:532
  94.8 18.9 %collective-permute-start.2 = (f32[2,128]{1,0:T(2,128)S(1)}, f32[2,128]{1,0:T(2,128)S(1)}, u32[]{:S(2)}, u32[]{:S(2)}) collective-permute-start(f32[2,128]{1,0:T(2,128)S(1)} %add.14), channel_id=1, source_target_pairs={{0,128},{32,160},{64,192},{96,224},{128,0},{160,32},{192,64},{224,... | collective-permute-start | bytes 3080 | tf_op jit(solution)/shard_map/ppermute | solution.py:532
  143.8 44.7 %all-to-all-start.1 = ((bf16[32,3,128,128]{3,2,1,0:T(8,128)(2,1)}), bf16[32,3,128,128]{3,2,1,0:T(8,128)(2,1)}, u32[]{:S(2)}, u32[]{:S(2)}) async-start(bf16[32,3,128,128]{3,2,1,0:T(8,128)(2,1)} %get-tuple-element.13), calls=%async_computation.1 | async-start | bytes 6291456 | tf_op jit(solution)/shard_map/all_to_all | solution.py:524

commit v4 on v3

--- a/solution.py
+++ b/solution.py
@@ -543,6 +543,7 @@
     returned = exchange(y)
     d_values = value_gradients(*tables, x, own_gains, lse)
     d_values = put_terms(d_values, sum_over_sequences(terms))
+    d_values, returned = lax.optimization_barrier((d_values, returned))
     out, d_queries, d_keys = join_heads(returned)
     place = lax.axis_index("dp").reshape(1)
     d_values, d_gains = join_heads_terms(place, exchange(d_values), gains.shape[1] // HD)

time: 192 us -> 162 us (0.84)
  blocking collectives: 52.4 us -> 24.3 us
  waiting for transfers between devices: 67.4 us -> 55.6 us
  starting transfers between devices: 24.4 us -> 31.7 us
    all_to_all x1 -> x0, blocking collectives: 28.1 us -> none  [exchange(): return lax.all_to_all(x, 'ctx', split_axis=0, concat_axis=0, tiled=True)]
    all_to_all x2 -> x3, waiting for transfers between devices: 65.5 us -> 53.1 us  [exchange(): return lax.all_to_all(x, 'ctx', split_axis=0, concat_axis=0, tiled=True)]
    all_to_all x2 -> x3, starting transfers between devices: 13.6 us -> 20.9 us  [exchange(): return lax.all_to_all(x, 'ctx', split_axis=0, concat_axis=0, tiled=True)]
  transfers between devices with their start and end apart: 5 -> 6, of which waited for: 4 -> 5; matrix products, arithmetic and copies ran while one was open for 0% -> 0% of each run, Pallas kernels for 8% -> 11%
where the time goes in v4:
time: 162 us
  waiting for transfers between devices  55.6 us (34%)
  Pallas kernels  46.6 us (29%)
  starting transfers between devices  31.7 us (20%)
  blocking collectives  24.3 us (15%)
  local copies, waits for them, and re-layouts  1.75 us (1%)
    all_to_all x3, waiting for transfers between devices, exchange(): return lax.all_to_all(x, 'ctx', split_axis=0, concat_axis=0, tiled=True)  53.1 us
    all_gather x1, blocking collectives, on_device(): all_gains = lax.all_gather(gains, 'dp', axis=1, tiled=True)  24.3 us
    pallas_call x1, Pallas kernels, attend_without_values(): pl.pallas_call(main_kernel, out_shape=(pltpu.HBM((blocks, 3, BLOCK, HD),...  24 us
    all_to_all x3, starting transfers between devices, exchange(): return lax.all_to_all(x, 'ctx', split_axis=0, concat_axis=0, tiled=True)  20.9 us
    pallas_call x1, Pallas kernels, value_gradients(): pl.pallas_call(values_kernel, out_shape=pltpu.HBM((blocks, BLOCK + TERM_R...  13.2 us
    ppermute x3, starting transfers between devices, sum_over_sequences(): terms = terms + lax.ppermute(terms, 'dp', pairs)  10.8 us
    pallas_call x1, Pallas kernels, split_heads(): pl.pallas_call(split_kernel, out_shape=pltpu.HBM((heads, 4, tokens, HD),...  3.43 us
  transfers between devices with their start and end apart: 6, of which 5 were waited for; matrix products, arithmetic and copies ran while one was open for 0% of the time, Pallas kernels for 11%

profile of v4, /device:TPU:1, one launch (start us, length us, event | category | flops | bytes accessed | tf_op | source)
XLA Modules:
  0.0 162.1 jit_solution(10523926932151261692)
XLA Ops:
  0.6 3.4 %split_heads.1 = bf16[32,4,128,128]{3,2,1,0:T(8,128)(2,1)} custom-call(bf16[1,128,4096]{2,1,0:T(8,128)(2,1)} %q_hbm.1, bf16[1,128,4096]{2,1,0:T(8,128)(2,1)} %k_hbm.1, bf16[1,128,4096]{2,1,0:T(8,128)(2,1)} %v_hbm.1, bf16[1,128,4096]{2,1,0:T(8,128)(2,1)} %d_hbm.1), custom_call_target="tpu_custom_call" | custom-call | tf_op jit(solution)/shard_map/split_heads/pallas_call | solution.py:426
  4.1 0.0 copy-start.3
  4.1 0.0 copy-start.2
  4.1 0.0 copy-start
  4.1 8.8 %all-to-all-start = ((bf16[32,4,128,128]{3,2,1,0:T(8,128)(2,1)}), bf16[32,4,128,128]{3,2,1,0:T(8,128)(2,1)}, u32[]{:S(2)}, u32[]{:S(2)}) async-start(bf16[32,4,128,128]{3,2,1,0:T(8,128)(2,1)} %split_heads.1), calls=%async_computation | async-start | bytes 8388608 | tf_op jit(solution)/shard_map/all_to_all | solution.py:524
  13.6 0.0 copy-done.3
  13.6 0.1 copy.15.random_ref
  13.7 0.0 copy-done.2
  13.7 24.3 %all_gather.3 = f32[2,4096]{1,0:T(2,128)S(1)} all-gather(f32[2,512]{1,0:T(2,128)S(1)} %copy-done.2), channel_id=1, replica_groups=mesh['dp'=8,'ctx'=32] {'dp'}, dimensions={1}, use_global_device_ids=true | all-gather | bytes 36864 | tf_op jit(solution)/shard_map/all_gather | solution.py:539
  37.9 27.2 %all-to-all-done.x_hbm = bf16[32,4,128,128]{3,2,1,0:T(8,128)(2,1)} async-done(((bf16[32,4,128,128]{3,2,1,0:T(8,128)(2,1)}), bf16[32,4,128,128]{3,2,1,0:T(8,128)(2,1)}, u32[]{:S(2)}, u32[]{:S(2)}) %all-to-all-start) | async-done | bytes 4194336 | tf_op jit(solution)/shard_map/all_to_all | solution.py:524
  65.1 0.0 copy-done
  65.1 24.0 %attend_without_values.1 = (bf16[32,3,128,128]{3,2,1,0:T(8,128)(2,1)}, f32[32,128,128]{2,1,0:T(8,128)}, f32[2,128]{1,0:T(2,128)S(1)}) custom-call(s32[1]{0:T(128)S(6)} %copy.17.width_ref, s32[1,2]{1,0:T(1,128)S(1)} %copy-done, s32[1,32,3]{2,1,0:T(8,128)S(1)} %copy.15.random_ref, bf16[32,4,128,128]{3,2,1,0:T(8,128)(2,1)} %all-to-all-done.x_hbm, ...), custom_call_target="tpu_custom_call" | custom-call | tf_op jit(solution)/shard_map/attend_without_values/pallas_call | solution.py:323
  89.1 7.1 %all-to-all-start.1 = ((bf16[32,3,128,128]{3,2,1,0:T(8,128)(2,1)}), bf16[32,3,128,128]{3,2,1,0:T(8,128)(2,1)S(1)}, u32[]{:S(2)}, u32[]{:S(2)}) async-start(bf16[32,3,128,128]{3,2,1,0:T(8,128)(2,1)} %get-tuple-element.17), calls=%async_computation.1 | async-start | bytes 6291456 | tf_op jit(solution)/shard_map/all_to_all | solution.py:524
  96.2 1.7 %collective-permute-start = (f32[2,128]{1,0:T(2,128)S(1)}, f32[2,128]{1,0:T(2,128)S(1)}, u32[]{:S(2)}, u32[]{:S(2)}) collective-permute-start(f32[2,128]{1,0:T(2,128)S(1)} %get-tuple-element.16), channel_id=1, source_target_pairs={{0,32},{32,0},{64,96},{96,64},{128,160},{160,128},{192,224},{224,1... | collective-permute-start | bytes 3080 | tf_op jit(solution)/shard_map/ppermute | solution.py:532
  98.0 1.3 collective-permute-done
  99.2 3.0 %collective-permute-start.1 = (f32[2,128]{1,0:T(2,128)S(1)}, f32[2,128]{1,0:T(2,128)S(1)}, u32[]{:S(2)}, u32[]{:S(2)}) collective-permute-start(f32[2,128]{1,0:T(2,128)S(1)} %add.13), channel_id=1, source_target_pairs={{0,64},{32,96},{64,0},{96,32},{128,192},{160,224},{192,128},{224,1... | collective-permute-start | bytes 3080 | tf_op jit(solution)/shard_map/ppermute | solution.py:532
  102.2 1.3 collective-permute-done.1
  103.5 6.1 %collective-permute-start.2 = (f32[2,128]{1,0:T(2,128)S(1)}, f32[2,128]{1,0:T(2,128)S(1)}, u32[]{:S(2)}, u32[]{:S(2)}) collective-permute-start(f32[2,128]{1,0:T(2,128)S(1)} %add.14), channel_id=1, source_target_pairs={{0,128},{32,160},{64,192},{96,224},{128,0},{160,32},{192,64},{224,... | collective-permute-start | bytes 3080 | tf_op jit(solution)/shard_map/ppermute | solution.py:532
  109.6 13.2 %value_gradients.1.y_in = bf16[32,136,128]{2,1,0:T(8,128)(2,1)} custom-call(s32[1]{0:T(128)S(6)} %copy.17.width_ref, s32[1,2]{1,0:T(1,128)S(1)} %copy-done, s32[1,32,3]{2,1,0:T(8,128)S(1)} %copy.15.random_ref, bf16[32,4,128,128]{3,2,1,0:T(8,128)(2,1)} %all-to-all-done.x_hbm, f32[2,128]{1,0:T(2,128)S(1)} %constant_dynamic-slice_fusion.gain_ref, ...), custom_call_target="tpu_custom_call" | custom-call | tf_op jit(solution)/shard_map/value_gradients/pallas_call | solution.py:351
  122.8 0.0 collective-permute-done.2
  122.8 0.6 add.15.total_ref
  123.4 1.4 put_terms.1
  124.7 11.3 %all-to-all-done.1.z_hbm = bf16[32,3,128,128]{3,2,1,0:T(8,128)(2,1)S(1)} async-done(((bf16[32,3,128,128]{3,2,1,0:T(8,128)(2,1)}), bf16[32,3,128,128]{3,2,1,0:T(8,128)(2,1)S(1)}, u32[]{:S(2)}, u32[]{:S(2)}) %all-to-all-start.1) | async-done | bytes 3145760 | tf_op jit(solution)/shard_map/all_to_all | solution.py:524
  136.0 0.0 copy-start.1
  136.0 1.6 %copy-done.1 = bf16[32,3,128,128]{3,2,1,0:T(8,128)(2,1)} copy-done((bf16[32,3,128,128]{3,2,1,0:T(8,128)(2,1)}, bf16[32,3,128,128]{3,2,1,0:T(8,128)(2,1)S(1)}, u32[]{:S(2)}) %copy-start.1) | copy-done | bytes 3145752
  137.6 5.0 %all-to-all-start.2 = ((bf16[32,136,128]{2,1,0:T(8,128)(2,1)}), bf16[32,136,128]{2,1,0:T(8,128)(2,1)S(1)}, u32[]{:S(2)}, u32[]{:S(2)}) async-start(bf16[32,136,128]{2,1,0:T(8,128)(2,1)} %put_terms.1), calls=%async_computation.2 | async-start | bytes 2228224 | tf_op jit(solution)/shard_map/all_to_all | solution.py:524
  142.6 3.0 %join_heads.1 = (bf16[1,128,4096]{2,1,0:T(8,128)(2,1)}, bf16[1,128,4096]{2,1,0:T(8,128)(2,1)}, bf16[1,128,4096]{2,1,0:T(8,128)(2,1)}) custom-call(bf16[32,3,128,128]{3,2,1,0:T(8,128)(2,1)} %copy-done.1), custom_call_target="tpu_custom_call" | custom-call | tf_op jit(solution)/shard_map/join_heads/pallas_call | solution.py:488
  145.6 14.6 %all-to-all-done.2.z_ref = bf16[32,136,128]{2,1,0:T(8,128)(2,1)S(1)} async-done(((bf16[32,136,128]{2,1,0:T(8,128)(2,1)}), bf16[32,136,128]{2,1,0:T(8,128)(2,1)S(1)}, u32[]{:S(2)}, u32[]{:S(2)}) %all-to-all-start.2) | async-done | bytes 1114144 | tf_op jit(solution)/shard_map/all_to_all | solution.py:524
  160.3 1.7 %join_heads_terms.1 = (bf16[1,128,4096]{2,1,0:T(8,128)(2,1)}, f32[2,512]{1,0:T(2,128)}) custom-call(s32[1]{0:T(128)} %bitcast.place_ref, bf16[32,136,128]{2,1,0:T(8,128)(2,1)S(1)} %all-to-all-done.2.z_ref), custom_call_target="tpu_custom_call" | custom-call | tf_op jit(solution)/shard_map/join_heads_terms/pallas_call | solution.py:506
  (3 shorter events, 0.0 us)
Async XLA Ops:
  4.1 9.5 %copy-start.3 = (s32[1,32,3]{1,0,2:T(1,128)S(1)}, s32[1,32,3]{1,0,2:T(1,128)}, u32[]{:S(2)}) copy-start(s32[1,32,3]{1,0,2:T(1,128)} %param.15) | copy-start | bytes 1156
  4.1 9.6 %copy-start.2 = (f32[2,512]{1,0:T(2,128)S(1)}, f32[2,512]{1,0:T(2,128)}, u32[]{:S(2)}) copy-start(f32[2,512]{1,0:T(2,128)} %param.12) | copy-start | bytes 12292
  4.1 61.0 %copy-start = (s32[1,2]{1,0:T(1,128)S(1)}, s32[1,2]{1,0:T(1,128)}, u32[]{:S(2)}) copy-start(s32[1,2]{1,0:T(1,128)} %global_ref.3) | copy-start | bytes 28
  4.1 61.0 %all-to-all-start = ((bf16[32,4,128,128]{3,2,1,0:T(8,128)(2,1)}), bf16[32,4,128,128]{3,2,1,0:T(8,128)(2,1)}, u32[]{:S(2)}, u32[]{:S(2)}) async-start(bf16[32,4,128,128]{3,2,1,0:T(8,128)(2,1)} %split_heads.1), calls=%async_computation | async-start | bytes 8388608 | tf_op jit(solution)/shard_map/all_to_all | solution.py:524
  89.1 46.9 %all-to-all-start.1 = ((bf16[32,3,128,128]{3,2,1,0:T(8,128)(2,1)}), bf16[32,3,128,128]{3,2,1,0:T(8,128)(2,1)S(1)}, u32[]{:S(2)}, u32[]{:S(2)}) async-start(bf16[32,3,128,128]{3,2,1,0:T(8,128)(2,1)} %get-tuple-element.17), calls=%async_computation.1 | async-start | bytes 6291456 | tf_op jit(solution)/shard_map/all_to_all | solution.py:524
  96.2 3.0 %collective-permute-start = (f32[2,128]{1,0:T(2,128)S(1)}, f32[2,128]{1,0:T(2,128)S(1)}, u32[]{:S(2)}, u32[]{:S(2)}) collective-permute-start(f32[2,128]{1,0:T(2,128)S(1)} %get-tuple-element.16), channel_id=1, source_target_pairs={{0,32},{32,0},{64,96},{96,64},{128,160},{160,128},{192,224},{224,1... | collective-permute-start | bytes 3080 | tf_op jit(solution)/shard_map/ppermute | solution.py:532
  99.2 4.2 %collective-permute-start.1 = (f32[2,128]{1,0:T(2,128)S(1)}, f32[2,128]{1,0:T(2,128)S(1)}, u32[]{:S(2)}, u32[]{:S(2)}) collective-permute-start(f32[2,128]{1,0:T(2,128)S(1)} %add.13), channel_id=1, source_target_pairs={{0,64},{32,96},{64,0},{96,32},{128,192},{160,224},{192,128},{224,1... | collective-permute-start | bytes 3080 | tf_op jit(solution)/shard_map/ppermute | solution.py:532
  103.5 19.3 %collective-permute-start.2 = (f32[2,128]{1,0:T(2,128)S(1)}, f32[2,128]{1,0:T(2,128)S(1)}, u32[]{:S(2)}, u32[]{:S(2)}) collective-permute-start(f32[2,128]{1,0:T(2,128)S(1)} %add.14), channel_id=1, source_target_pairs={{0,128},{32,160},{64,192},{96,224},{128,0},{160,32},{192,64},{224,... | collective-permute-start | bytes 3080 | tf_op jit(solution)/shard_map/ppermute | solution.py:532
  136.0 1.6 %copy-start.1 = (bf16[32,3,128,128]{3,2,1,0:T(8,128)(2,1)}, bf16[32,3,128,128]{3,2,1,0:T(8,128)(2,1)S(1)}, u32[]{:S(2)}) copy-start(bf16[32,3,128,128]{3,2,1,0:T(8,128)(2,1)S(1)} %all-to-all-done.1.z_hbm) | copy-start | bytes 9437188
  137.6 22.6 %all-to-all-start.2 = ((bf16[32,136,128]{2,1,0:T(8,128)(2,1)}), bf16[32,136,128]{2,1,0:T(8,128)(2,1)S(1)}, u32[]{:S(2)}, u32[]{:S(2)}) async-start(bf16[32,136,128]{2,1,0:T(8,128)(2,1)} %put_terms.1), calls=%async_computation.2 | async-start | bytes 2228224 | tf_op jit(solution)/shard_map/all_to_all | solution.py:524

commit v5 on v4

--- a/solution.py
+++ b/solution.py
@@ -15,7 +15,7 @@
 SCALE_LOG2 = SCALE * LOG2E
 PENALTY = 1e30
 CHUNK = 8
-GROUP = 5
+GROUP = 10
 PARTS = 4
 TERM_ROWS = 8
 MIB = 1024 * 1024
@@ -75,6 +75,12 @@
     return ids, penalties
 
 
+def split_slots(i, width_ref, global_ref, random_ref, block_count):
+    ids, penalties = key_slots(i, width_ref, global_ref, random_ref, block_count)
+    own = [0, 1, 2] + list(range(5, len(ids)))
+    return [ids[t] for t in own], [penalties[t] for t in own], penalties[3:5]
+
+
 def sparse_blocks(step, group, global_ref):
     low = jnp.minimum(global_ref[0, 0], global_ref[0, 1])
     high = jnp.maximum(global_ref[0, 0], global_ref[0, 1])
@@ -111,7 +117,7 @@
 
 def main_kernel(
     width_ref, global_ref, random_ref, x_hbm, gain_ref, y_hbm, lse_hbm, terms_ref,
-    x_ref, ks_ref, p_ref, dk_ref, y_ref, lse_ref, tq_ref, in_sems, out_sems, lse_sem,
+    x_ref, ks_ref, p_ref, dk_ref, y_ref, lse_ref, tq_ref, in_sems, out_sems, row_sem, lse_sem,
 ):
     copies = load_all(x_hbm, x_ref, in_sems)
     block_count = ks_ref.shape[0]
@@ -175,60 +181,89 @@
     terms = dq * q_raw
     tq_ref[...] = terms[:BLOCK] + terms[BLOCK:]
 
+    def send_block(i):
+        pltpu.make_async_copy(y_ref.at[i, pl.ds(0, 2)], y_hbm.at[i, pl.ds(0, 2)], row_sem).start()
+        pltpu.make_async_copy(lse_ref.at[i], lse_hbm.at[i], lse_sem).start()
+
+    send_block(g0)
+    send_block(g1)
+
     def step(n, carry):
         blocks = sparse_blocks(n, GROUP, global_ref)
         us = range(GROUP)
-        slots = [key_slots(i, width_ref, global_ref, random_ref, block_count) for i in blocks]
+        slots = [split_slots(i, width_ref, global_ref, random_ref, block_count) for i in blocks]
         k_slots = [jnp.concatenate([ks_ref[t] for t in slots[u][0]], 0) for u in us]
         v_slots = [jnp.concatenate([v_ref[t] for t in slots[u][0]], 0) for u in us]
+        k_global = pair(ks_ref, g0, g1)
+        v_global = pair(v_ref, g0, g1)
+
+        def rows_of(stacked, u):
+            return stacked[u * BLOCK : (u + 1) * BLOCK]
+
         q_raw = [q_ref[i].astype(F32) for i in blocks]
         q_scaled = [(q * gain_q).astype(BF16) for q in q_raw]
+        q_all = jnp.concatenate(q_scaled, 0)
         d_out = [d_ref[i] for i in blocks]
         scores = [dot_nt(q_scaled[u], k_slots[u]) for u in us]
+        scores_global = dot_nt(q_all, k_global)
         dps = [dot_nt(d_out[u], v_slots[u]) for u in us]
+        dps_global = dot_nt(jnp.concatenate(d_out, 0), v_global)
+
+        def tiles(own, shared, u):
+            own_tiles = [slot_of(own[u], t) for t in range(own[u].shape[1] // BLOCK)]
+            return own_tiles + [slot_of(rows_of(shared, u), t) for t in range(2)]
+
+        s_tiles = [tiles(scores, scores_global, u) for u in us]
+        d_tiles = [tiles(dps, dps_global, u) for u in us]
         tops = [
-            jnp.max(lane_fold(jnp.maximum, scores[u]), axis=1, keepdims=True) * SCALE_LOG2
+            jnp.max(functools.reduce(jnp.maximum, s_tiles[u]), axis=1, keepdims=True) * SCALE_LOG2
             for u in us
         ]
         es = [
             [
-                jnp.exp2(slot_of(scores[u], t) * SCALE_LOG2 - (tops[u] + penalty))
-                for t, penalty in enumerate(slots[u][1])
+                jnp.exp2(tile * SCALE_LOG2 - (tops[u] + penalty))
+                for tile, penalty in zip(s_tiles[u], slots[u][1] + slots[u][2])
             ]
             for u in us
         ]
         totals = [row_sum(functools.reduce(jnp.add, es[u])) for u in us]
         inverses = [1.0 / totals[u] for u in us]
         ps = [[e * inverses[u] for e in es[u]] for u in us]
-        p_b = [jnp.concatenate([p.astype(BF16) for p in ps[u]], 1) for u in us]
-        outs = [dot_nn(p_b[u], v_slots[u]).astype(BF16) for u in us]
+        p_b = [[p.astype(BF16) for p in ps[u]] for u in us]
+        out_global = dot_nn(
+            jnp.concatenate([jnp.concatenate(p_b[u][-2:], 1) for u in us], 0), v_global
+        )
+        outs = [
+            (dot_nn(jnp.concatenate(p_b[u][:-2], 1), v_slots[u]) + rows_of(out_global, u)).astype(BF16)
+            for u in us
+        ]
         row_dots = [row_sum(d_out[u].astype(F32) * outs[u].astype(F32)) for u in us]
         ds = [
-            jnp.concatenate(
-                [
-                    (p * (slot_of(dps[u], t) - row_dots[u])).astype(BF16)
-                    for t, p in enumerate(ps[u])
-                ],
-                1,
-            )
+            [(p * (tile - row_dots[u])).astype(BF16) for p, tile in zip(ps[u], d_tiles[u])]
             for u in us
         ]
-        dqs = [dot_nn(ds[u], k_slots[u]) * SCALE for u in us]
-        dk_t = [dot_tn(q_scaled[u], ds[u]) for u in us]
+        ds_own = [jnp.concatenate(ds[u][:-2], 1) for u in us]
+        ds_global = jnp.concatenate([jnp.concatenate(ds[u][-2:], 1) for u in us], 0)
+        dq_global = dot_nn(ds_global, k_global)
+        dqs = [(dot_nn(ds_own[u], k_slots[u]) + rows_of(dq_global, u)) * SCALE for u in us]
+        dk_t = [dot_tn(q_scaled[u], ds_own[u]) for u in us]
+        dk_global = dot_tn(q_all, ds_global)
         for u in us:
             y_ref[blocks[u], 0] = outs[u]
             y_ref[blocks[u], 1] = (dqs[u] * gain_q).astype(BF16)
             lse_ref[blocks[u]] = jnp.broadcast_to(
                 tops[u] + jnp.log(totals[u]) * LOG2E, (BLOCK, BLOCK)
             )
+            send_block(blocks[u])
         tq_ref[...] += functools.reduce(jnp.add, [dqs[u] * q_raw[u] for u in us])
         for u in us:
             for t, block_id in enumerate(slots[u][0]):
                 dk_ref[block_id] += slot_of(dk_t[u], t)
+        dk_ref[g0] += slot_of(dk_global, 0)
+        dk_ref[g1] += slot_of(dk_global, 1)
         return carry
 
     lax.fori_loop(0, (block_count - 2) // GROUP, step, 0)
-    lse_copy = pltpu.make_async_copy(lse_ref, lse_hbm, lse_sem)
 
     def finish(j, acc):
         dk = dk_ref[j].T * SCALE
@@ -241,14 +276,16 @@
     for part in range(PARTS):
         tk = lax.fori_loop(part * size, (part + 1) * size, finish, tk, unroll=True)
         rows = pl.ds(part * size, size)
-        out_copies.append(pltpu.make_async_copy(y_ref.at[rows], y_hbm.at[rows], out_sems.at[part]))
+        src, dst = y_ref.at[rows, 2], y_hbm.at[rows, 2]
+        out_copies.append(pltpu.make_async_copy(src, dst, out_sems.at[part]))
         out_copies[-1].start()
-    lse_copy.start()
     terms_ref[0:1, :] = jnp.sum(tq_ref[...], axis=0, keepdims=True)
     terms_ref[1:2, :] = jnp.sum(tk, axis=0, keepdims=True)
     for copy in out_copies:
         copy.wait()
-    lse_copy.wait()
+    first = pl.ds(0, 2)
+    pltpu.make_async_copy(y_ref.at[:, first], y_hbm.at[:, first], row_sem).wait()
+    pltpu.make_async_copy(lse_ref, lse_hbm, lse_sem).wait()
 
 
 def values_kernel(
@@ -340,6 +377,7 @@
             pltpu.SemaphoreType.DMA((4,)),
             pltpu.SemaphoreType.DMA((PARTS,)),
             pltpu.SemaphoreType.DMA,
+            pltpu.SemaphoreType.DMA,
         ],
         compiler_params=pltpu.CompilerParams(vmem_limit_bytes=40 * MIB),
         name="attend_without_values",
@@ -363,7 +401,7 @@
             pltpu.SemaphoreType.DMA,
             pltpu.SemaphoreType.DMA,
         ],
-        compiler_params=pltpu.CompilerParams(vmem_limit_bytes=40 * MIB),
+        compiler_params=pltpu.CompilerParams(vmem_limit_bytes=62 * MIB),
         name="value_gradients",
     )(widths, global_ids, random_ids, *in_hbm(x), gains, *in_hbm(lse))
 

time: 162 us -> 159 us (0.981)
  Pallas kernels: 46.6 us -> 43.4 us
  local copies, waits for them, and re-layouts: 1.75 us -> 0.12 us
    pallas_call x1, Pallas kernels: 24 us -> 21.4 us  [attend_without_values(): pl.pallas_call(main_kernel, out_shape=(pltpu.HBM((blocks, 3, BLOCK, HD),...]
    unnamed x9 -> x11, local copies, waits for them, and re-layouts: 1.75 us -> 0.12 us
where the time goes in v5:
time: 159 us; the launch traced here: 158 us
  waiting for transfers between devices  56.3 us (35%)
  Pallas kernels  43.4 us (27%)
  starting transfers between devices  31.8 us (20%)
  blocking collectives  24.3 us (15%)
  between operations  1.59 us (1%)
    all_to_all x3, waiting for transfers between devices, exchange(): return lax.all_to_all(x, 'ctx', split_axis=0, concat_axis=0, tiled=True)  53.6 us
    all_gather x1, blocking collectives, on_device(): all_gains = lax.all_gather(gains, 'dp', axis=1, tiled=True)  24.3 us
    pallas_call x1, Pallas kernels, attend_without_values(): pl.pallas_call(main_kernel, out_shape=(pltpu.HBM((blocks, 3, BLOCK, HD),...  21.4 us
    all_to_all x3, starting transfers between devices, exchange(): return lax.all_to_all(x, 'ctx', split_axis=0, concat_axis=0, tiled=True)  20.9 us
    pallas_call x1, Pallas kernels, value_gradients(): pl.pallas_call(values_kernel, out_shape=pltpu.HBM((blocks, BLOCK + TERM_R...  12.6 us
    ppermute x3, starting transfers between devices, sum_over_sequences(): terms = terms + lax.ppermute(terms, 'dp', pairs)  10.8 us
    pallas_call x1, Pallas kernels, split_heads(): pl.pallas_call(split_kernel, out_shape=pltpu.HBM((heads, 4, tokens, HD),...  3.46 us
  transfers between devices with their start and end apart: 6, of which 5 were waited for; matrix products, arithmetic and copies ran while one was open for 0% of the time, Pallas kernels for 11%

profile of v5, /device:TPU:1, one launch (start us, length us, event | category | flops | bytes accessed | tf_op | source)
XLA Modules:
  0.0 158.1 jit_solution(5842288703711901119)
XLA Ops:
  0.6 3.5 %split_heads.1 = bf16[32,4,128,128]{3,2,1,0:T(8,128)(2,1)} custom-call(bf16[1,128,4096]{2,1,0:T(8,128)(2,1)} %q_hbm.1, bf16[1,128,4096]{2,1,0:T(8,128)(2,1)} %k_hbm.1, bf16[1,128,4096]{2,1,0:T(8,128)(2,1)} %v_hbm.1, bf16[1,128,4096]{2,1,0:T(8,128)(2,1)} %d_hbm.1), custom_call_target="tpu_custom_call" | custom-call | tf_op jit(solution)/shard_map/split_heads/pallas_call | solution.py:464
  4.1 0.0 copy-start.4
  4.1 0.0 copy-start.3
  4.1 0.0 copy-start.2
  4.1 8.8 %all-to-all-start = ((bf16[32,4,128,128]{3,2,1,0:T(8,128)(2,1)}), bf16[32,4,128,128]{3,2,1,0:T(8,128)(2,1)}, u32[]{:S(2)}, u32[]{:S(2)}) async-start(bf16[32,4,128,128]{3,2,1,0:T(8,128)(2,1)} %split_heads.1), calls=%async_computation | async-start | bytes 8388608 | tf_op jit(solution)/shard_map/all_to_all | solution.py:562
  13.6 0.0 copy-done.4
  13.6 0.1 copy.15.random_ref
  13.7 0.0 copy-start
  13.7 0.0 copy-done.3
  13.7 24.3 %all_gather.3 = f32[2,4096]{1,0:T(2,128)S(1)} all-gather(f32[2,512]{1,0:T(2,128)S(1)} %copy-done.3), channel_id=1, replica_groups=mesh['dp'=8,'ctx'=32] {'dp'}, dimensions={1}, use_global_device_ids=true | all-gather | bytes 36864 | tf_op jit(solution)/shard_map/all_gather | solution.py:577
  38.0 0.0 copy-start.1
  38.0 27.2 %all-to-all-done.x_hbm = bf16[32,4,128,128]{3,2,1,0:T(8,128)(2,1)} async-done(((bf16[32,4,128,128]{3,2,1,0:T(8,128)(2,1)}), bf16[32,4,128,128]{3,2,1,0:T(8,128)(2,1)}, u32[]{:S(2)}, u32[]{:S(2)}) %all-to-all-start) | async-done | bytes 4194336 | tf_op jit(solution)/shard_map/all_to_all | solution.py:562
  65.1 0.0 copy-done.2
  65.2 21.4 %attend_without_values.1 = (bf16[32,3,128,128]{3,2,1,0:T(8,128)(2,1)}, f32[32,128,128]{2,1,0:T(8,128)}, f32[2,128]{1,0:T(2,128)S(1)}) custom-call(s32[1]{0:T(128)S(6)} %copy.17.width_ref, s32[1,2]{1,0:T(1,128)S(1)} %copy-done.2, s32[1,32,3]{2,1,0:T(8,128)S(1)} %copy.15.random_ref, bf16[32,4,128,128]{3,2,1,0:T(8,128)(2,1)} %all-to-all-done.x_hbm, ...), custom_call_target="tpu_custom_call" | custom-call | tf_op jit(solution)/shard_map/attend_without_values/pallas_call | solution.py:360
  86.6 0.0 copy-done
  86.6 0.0 copy-done.1
  86.6 7.2 %all-to-all-start.1 = ((bf16[32,3,128,128]{3,2,1,0:T(8,128)(2,1)}), bf16[32,3,128,128]{3,2,1,0:T(8,128)(2,1)}, u32[]{:S(2)}, u32[]{:S(2)}) async-start(bf16[32,3,128,128]{3,2,1,0:T(8,128)(2,1)} %get-tuple-element.17), calls=%async_computation.1 | async-start | bytes 6291456 | tf_op jit(solution)/shard_map/all_to_all | solution.py:562
  93.8 1.7 %collective-permute-start = (f32[2,128]{1,0:T(2,128)S(1)}, f32[2,128]{1,0:T(2,128)S(1)}, u32[]{:S(2)}, u32[]{:S(2)}) collective-permute-start(f32[2,128]{1,0:T(2,128)S(1)} %get-tuple-element.16), channel_id=1, source_target_pairs={{0,32},{32,0},{64,96},{96,64},{128,160},{160,128},{192,224},{224,1... | collective-permute-start | bytes 3080 | tf_op jit(solution)/shard_map/ppermute | solution.py:570
  95.5 1.4 collective-permute-done
  96.9 3.0 %collective-permute-start.1 = (f32[2,128]{1,0:T(2,128)S(1)}, f32[2,128]{1,0:T(2,128)S(1)}, u32[]{:S(2)}, u32[]{:S(2)}) collective-permute-start(f32[2,128]{1,0:T(2,128)S(1)} %add.13), channel_id=1, source_target_pairs={{0,64},{32,96},{64,0},{96,32},{128,192},{160,224},{192,128},{224,1... | collective-permute-start | bytes 3080 | tf_op jit(solution)/shard_map/ppermute | solution.py:570
  99.9 1.4 collective-permute-done.1
  101.2 6.1 %collective-permute-start.2 = (f32[2,128]{1,0:T(2,128)S(1)}, f32[2,128]{1,0:T(2,128)S(1)}, u32[]{:S(2)}, u32[]{:S(2)}) collective-permute-start(f32[2,128]{1,0:T(2,128)S(1)} %add.14), channel_id=1, source_target_pairs={{0,128},{32,160},{64,192},{96,224},{128,0},{160,32},{192,64},{224,... | collective-permute-start | bytes 3080 | tf_op jit(solution)/shard_map/ppermute | solution.py:570
  107.3 12.6 %value_gradients.1.y_in = bf16[32,136,128]{2,1,0:T(8,128)(2,1)} custom-call(s32[1]{0:T(128)S(6)} %copy.17.width_ref, s32[1,2]{1,0:T(1,128)} %global_ref.3, s32[1,32,3]{2,1,0:T(8,128)} %copy-done, bf16[32,4,128,128]{3,2,1,0:T(8,128)(2,1)} %all-to-all-done.x_hbm, f32[2,128]{1,0:T(2,128)} %copy-done.1, f32[32,128,128]{2,1,0:T(8,128)} %get-tuple-element.15.lse_hbm), custom_call_target="tpu_custom_call" | custom-call | tf_op jit(solution)/shard_map/value_gradients/pallas_call | solution.py:389
  119.9 0.0 collective-permute-done.2
  119.9 0.6 add.15.total_ref
  120.5 1.3 put_terms.1
  121.8 11.8 %all-to-all-done.1.z_hbm = bf16[32,3,128,128]{3,2,1,0:T(8,128)(2,1)} async-done(((bf16[32,3,128,128]{3,2,1,0:T(8,128)(2,1)}), bf16[32,3,128,128]{3,2,1,0:T(8,128)(2,1)}, u32[]{:S(2)}, u32[]{:S(2)}) %all-to-all-start.1) | async-done | bytes 3145760 | tf_op jit(solution)/shard_map/all_to_all | solution.py:562
  133.6 5.0 %all-to-all-start.2 = ((bf16[32,136,128]{2,1,0:T(8,128)(2,1)}), bf16[32,136,128]{2,1,0:T(8,128)(2,1)S(1)}, u32[]{:S(2)}, u32[]{:S(2)}) async-start(bf16[32,136,128]{2,1,0:T(8,128)(2,1)} %put_terms.1), calls=%async_computation.2 | async-start | bytes 2228224 | tf_op jit(solution)/shard_map/all_to_all | solution.py:562
  138.6 3.0 %join_heads.1 = (bf16[1,128,4096]{2,1,0:T(8,128)(2,1)}, bf16[1,128,4096]{2,1,0:T(8,128)(2,1)}, bf16[1,128,4096]{2,1,0:T(8,128)(2,1)}) custom-call(bf16[32,3,128,128]{3,2,1,0:T(8,128)(2,1)} %all-to-all-done.1.z_hbm), custom_call_target="tpu_custom_call" | custom-call | tf_op jit(solution)/shard_map/join_heads/pallas_call | solution.py:526
  141.6 14.6 %all-to-all-done.2.z_ref = bf16[32,136,128]{2,1,0:T(8,128)(2,1)S(1)} async-done(((bf16[32,136,128]{2,1,0:T(8,128)(2,1)}), bf16[32,136,128]{2,1,0:T(8,128)(2,1)S(1)}, u32[]{:S(2)}, u32[]{:S(2)}) %all-to-all-start.2) | async-done | bytes 1114144 | tf_op jit(solution)/shard_map/all_to_all | solution.py:562
  156.2 1.7 %join_heads_terms.1 = (bf16[1,128,4096]{2,1,0:T(8,128)(2,1)}, f32[2,512]{1,0:T(2,128)}) custom-call(s32[1]{0:T(128)} %bitcast.place_ref, bf16[32,136,128]{2,1,0:T(8,128)(2,1)S(1)} %all-to-all-done.2.z_ref), custom_call_target="tpu_custom_call" | custom-call | tf_op jit(solution)/shard_map/join_heads_terms/pallas_call | solution.py:544
  (3 shorter events, 0.0 us)
Async XLA Ops:
  4.1 9.5 %copy-start.4 = (s32[1,32,3]{1,0,2:T(1,128)S(1)}, s32[1,32,3]{1,0,2:T(1,128)}, u32[]{:S(2)}) copy-start(s32[1,32,3]{1,0,2:T(1,128)} %param.15) | copy-start | bytes 1156
  4.1 9.6 %copy-start.3 = (f32[2,512]{1,0:T(2,128)S(1)}, f32[2,512]{1,0:T(2,128)}, u32[]{:S(2)}) copy-start(f32[2,512]{1,0:T(2,128)} %param.12) | copy-start | bytes 12292
  4.1 61.0 %copy-start.2 = (s32[1,2]{1,0:T(1,128)S(1)}, s32[1,2]{1,0:T(1,128)}, u32[]{:S(2)}) copy-start(s32[1,2]{1,0:T(1,128)} %global_ref.3) | copy-start | bytes 28
  4.1 61.0 %all-to-all-start = ((bf16[32,4,128,128]{3,2,1,0:T(8,128)(2,1)}), bf16[32,4,128,128]{3,2,1,0:T(8,128)(2,1)}, u32[]{:S(2)}, u32[]{:S(2)}) async-start(bf16[32,4,128,128]{3,2,1,0:T(8,128)(2,1)} %split_heads.1), calls=%async_computation | async-start | bytes 8388608 | tf_op jit(solution)/shard_map/all_to_all | solution.py:562
  13.7 72.9 %copy-start = (s32[1,32,3]{2,1,0:T(8,128)}, s32[1,32,3]{2,1,0:T(8,128)S(1)}, u32[]{:S(2)}) copy-start(s32[1,32,3]{2,1,0:T(8,128)S(1)} %copy.15.random_ref) | copy-start | bytes 1156
  38.0 48.6 %copy-start.1 = (f32[2,128]{1,0:T(2,128)}, f32[2,128]{1,0:T(2,128)S(1)}, u32[]{:S(2)}) copy-start(f32[2,128]{1,0:T(2,128)S(1)} %constant_dynamic-slice_fusion.gain_ref) | copy-start | bytes 3076
  86.6 47.0 %all-to-all-start.1 = ((bf16[32,3,128,128]{3,2,1,0:T(8,128)(2,1)}), bf16[32,3,128,128]{3,2,1,0:T(8,128)(2,1)}, u32[]{:S(2)}, u32[]{:S(2)}) async-start(bf16[32,3,128,128]{3,2,1,0:T(8,128)(2,1)} %get-tuple-element.17), calls=%async_computation.1 | async-start | bytes 6291456 | tf_op jit(solution)/shard_map/all_to_all | solution.py:562
  93.8 3.1 %collective-permute-start = (f32[2,128]{1,0:T(2,128)S(1)}, f32[2,128]{1,0:T(2,128)S(1)}, u32[]{:S(2)}, u32[]{:S(2)}) collective-permute-start(f32[2,128]{1,0:T(2,128)S(1)} %get-tuple-element.16), channel_id=1, source_target_pairs={{0,32},{32,0},{64,96},{96,64},{128,160},{160,128},{192,224},{224,1... | collective-permute-start | bytes 3080 | tf_op jit(solution)/shard_map/ppermute | solution.py:570
  96.9 4.3 %collective-permute-start.1 = (f32[2,128]{1,0:T(2,128)S(1)}, f32[2,128]{1,0:T(2,128)S(1)}, u32[]{:S(2)}, u32[]{:S(2)}) collective-permute-start(f32[2,128]{1,0:T(2,128)S(1)} %add.13), channel_id=1, source_target_pairs={{0,64},{32,96},{64,0},{96,32},{128,192},{160,224},{192,128},{224,1... | collective-permute-start | bytes 3080 | tf_op jit(solution)/shard_map/ppermute | solution.py:570
  101.2 18.7 %collective-permute-start.2 = (f32[2,128]{1,0:T(2,128)S(1)}, f32[2,128]{1,0:T(2,128)S(1)}, u32[]{:S(2)}, u32[]{:S(2)}) collective-permute-start(f32[2,128]{1,0:T(2,128)S(1)} %add.14), channel_id=1, source_target_pairs={{0,128},{32,160},{64,192},{96,224},{128,0},{160,32},{192,64},{224,... | collective-permute-start | bytes 3080 | tf_op jit(solution)/shard_map/ppermute | solution.py:570
  133.6 22.6 %all-to-all-start.2 = ((bf16[32,136,128]{2,1,0:T(8,128)(2,1)}), bf16[32,136,128]{2,1,0:T(8,128)(2,1)S(1)}, u32[]{:S(2)}, u32[]{:S(2)}) async-start(bf16[32,136,128]{2,1,0:T(8,128)(2,1)} %put_terms.1), calls=%async_computation.2 | async-start | bytes 2228224 | tf_op jit(solution)/shard_map/all_to_all | solution.py:562

commit v6 on v5

--- a/solution.py
+++ b/solution.py
@@ -14,7 +14,7 @@
 LOG2E = math.log2(math.e)
 SCALE_LOG2 = SCALE * LOG2E
 PENALTY = 1e30
-CHUNK = 8
+CHUNK = 32
 GROUP = 10
 PARTS = 4
 TERM_ROWS = 8

time: 159 us -> 158 us (level)
  transfers between devices with their start and end apart: 6 -> 6, of which waited for: 5 -> 5; matrix products, arithmetic and copies ran while one was open for 0% -> 0% of each run, Pallas kernels for 11% -> 10%
where the time goes in v6:
time: 158 us
  waiting for transfers between devices  56.9 us (36%)
  Pallas kernels  42.4 us (27%)
  starting transfers between devices  31.8 us (20%)
  blocking collectives  24.3 us (15%)
  between operations  1.59 us (1%)
    all_to_all x3, waiting for transfers between devices, exchange(): return lax.all_to_all(x, 'ctx', split_axis=0, concat_axis=0, tiled=True)  54.2 us
    all_gather x1, blocking collectives, on_device(): all_gains = lax.all_gather(gains, 'dp', axis=1, tiled=True)  24.3 us
    pallas_call x1, Pallas kernels, attend_without_values(): pl.pallas_call(main_kernel, out_shape=(pltpu.HBM((blocks, 3, BLOCK, HD),...  21 us
    all_to_all x3, starting transfers between devices, exchange(): return lax.all_to_all(x, 'ctx', split_axis=0, concat_axis=0, tiled=True)  20.9 us
    pallas_call x1, Pallas kernels, value_gradients(): pl.pallas_call(values_kernel, out_shape=pltpu.HBM((blocks, BLOCK + TERM_R...  12 us
    ppermute x3, starting transfers between devices, sum_over_sequences(): terms = terms + lax.ppermute(terms, 'dp', pairs)  10.8 us
    pallas_call x1, Pallas kernels, split_heads(): pl.pallas_call(split_kernel, out_shape=pltpu.HBM((heads, 4, tokens, HD),...  3.46 us
  transfers between devices with their start and end apart: 6, of which 5 were waited for; matrix products, arithmetic and copies ran while one was open for 0% of the time, Pallas kernels for 10%

profile of v6, /device:TPU:1, one launch (start us, length us, event | category | flops | bytes accessed | tf_op | source)
XLA Modules:
  0.0 157.6 jit_solution(10169667902982095549)
XLA Ops:
  0.6 3.5 %split_heads.1 = bf16[32,4,128,128]{3,2,1,0:T(8,128)(2,1)} custom-call(bf16[1,128,4096]{2,1,0:T(8,128)(2,1)} %q_hbm.1, bf16[1,128,4096]{2,1,0:T(8,128)(2,1)} %k_hbm.1, bf16[1,128,4096]{2,1,0:T(8,128)(2,1)} %v_hbm.1, bf16[1,128,4096]{2,1,0:T(8,128)(2,1)} %d_hbm.1), custom_call_target="tpu_custom_call" | custom-call | tf_op jit(solution)/shard_map/split_heads/pallas_call | solution.py:464
  4.1 0.0 copy-start.4
  4.1 0.0 copy-start.3
  4.1 0.0 copy-start.2
  4.1 8.8 %all-to-all-start = ((bf16[32,4,128,128]{3,2,1,0:T(8,128)(2,1)}), bf16[32,4,128,128]{3,2,1,0:T(8,128)(2,1)}, u32[]{:S(2)}, u32[]{:S(2)}) async-start(bf16[32,4,128,128]{3,2,1,0:T(8,128)(2,1)} %split_heads.1), calls=%async_computation | async-start | bytes 8388608 | tf_op jit(solution)/shard_map/all_to_all | solution.py:562
  13.6 0.0 copy-done.4
  13.6 0.1 copy.15.random_ref
  13.7 0.0 copy-start
  13.7 0.0 copy-done.3
  13.7 24.3 %all_gather.3 = f32[2,4096]{1,0:T(2,128)S(1)} all-gather(f32[2,512]{1,0:T(2,128)S(1)} %copy-done.3), channel_id=1, replica_groups=mesh['dp'=8,'ctx'=32] {'dp'}, dimensions={1}, use_global_device_ids=true | all-gather | bytes 36864 | tf_op jit(solution)/shard_map/all_gather | solution.py:577
  38.0 0.0 copy-start.1
  38.0 27.2 %all-to-all-done.x_hbm = bf16[32,4,128,128]{3,2,1,0:T(8,128)(2,1)} async-done(((bf16[32,4,128,128]{3,2,1,0:T(8,128)(2,1)}), bf16[32,4,128,128]{3,2,1,0:T(8,128)(2,1)}, u32[]{:S(2)}, u32[]{:S(2)}) %all-to-all-start) | async-done | bytes 4194336 | tf_op jit(solution)/shard_map/all_to_all | solution.py:562
  65.1 0.0 copy-done.2
  65.2 21.0 %attend_without_values.1 = (bf16[32,3,128,128]{3,2,1,0:T(8,128)(2,1)}, f32[32,128,128]{2,1,0:T(8,128)}, f32[2,128]{1,0:T(2,128)S(1)}) custom-call(s32[1]{0:T(128)S(6)} %copy.17.width_ref, s32[1,2]{1,0:T(1,128)S(1)} %copy-done.2, s32[1,32,3]{2,1,0:T(8,128)S(1)} %copy.15.random_ref, bf16[32,4,128,128]{3,2,1,0:T(8,128)(2,1)} %all-to-all-done.x_hbm, ...), custom_call_target="tpu_custom_call" | custom-call | tf_op jit(solution)/shard_map/attend_without_values/pallas_call | solution.py:360
  86.1 0.0 copy-done
  86.1 0.0 copy-done.1
  86.1 7.2 %all-to-all-start.1 = ((bf16[32,3,128,128]{3,2,1,0:T(8,128)(2,1)}), bf16[32,3,128,128]{3,2,1,0:T(8,128)(2,1)}, u32[]{:S(2)}, u32[]{:S(2)}) async-start(bf16[32,3,128,128]{3,2,1,0:T(8,128)(2,1)} %get-tuple-element.17), calls=%async_computation.1 | async-start | bytes 6291456 | tf_op jit(solution)/shard_map/all_to_all | solution.py:562
  93.3 1.7 %collective-permute-start = (f32[2,128]{1,0:T(2,128)S(1)}, f32[2,128]{1,0:T(2,128)S(1)}, u32[]{:S(2)}, u32[]{:S(2)}) collective-permute-start(f32[2,128]{1,0:T(2,128)S(1)} %get-tuple-element.16), channel_id=1, source_target_pairs={{0,32},{32,0},{64,96},{96,64},{128,160},{160,128},{192,224},{224,1... | collective-permute-start | bytes 3080 | tf_op jit(solution)/shard_map/ppermute | solution.py:570
  95.1 1.4 collective-permute-done
  96.4 3.0 %collective-permute-start.1 = (f32[2,128]{1,0:T(2,128)S(1)}, f32[2,128]{1,0:T(2,128)S(1)}, u32[]{:S(2)}, u32[]{:S(2)}) collective-permute-start(f32[2,128]{1,0:T(2,128)S(1)} %add.13), channel_id=1, source_target_pairs={{0,64},{32,96},{64,0},{96,32},{128,192},{160,224},{192,128},{224,1... | collective-permute-start | bytes 3080 | tf_op jit(solution)/shard_map/ppermute | solution.py:570
  99.4 1.4 collective-permute-done.1
  100.8 6.1 %collective-permute-start.2 = (f32[2,128]{1,0:T(2,128)S(1)}, f32[2,128]{1,0:T(2,128)S(1)}, u32[]{:S(2)}, u32[]{:S(2)}) collective-permute-start(f32[2,128]{1,0:T(2,128)S(1)} %add.14), channel_id=1, source_target_pairs={{0,128},{32,160},{64,192},{96,224},{128,0},{160,32},{192,64},{224,... | collective-permute-start | bytes 3080 | tf_op jit(solution)/shard_map/ppermute | solution.py:570
  106.9 12.0 %value_gradients.1.y_in = bf16[32,136,128]{2,1,0:T(8,128)(2,1)} custom-call(s32[1]{0:T(128)S(6)} %copy.17.width_ref, s32[1,2]{1,0:T(1,128)} %global_ref.3, s32[1,32,3]{2,1,0:T(8,128)} %copy-done, bf16[32,4,128,128]{3,2,1,0:T(8,128)(2,1)} %all-to-all-done.x_hbm, f32[2,128]{1,0:T(2,128)} %copy-done.1, f32[32,128,128]{2,1,0:T(8,128)} %get-tuple-element.15.lse_hbm), custom_call_target="tpu_custom_call" | custom-call | tf_op jit(solution)/shard_map/value_gradients/pallas_call | solution.py:389
  118.9 0.0 collective-permute-done.2
  118.9 0.6 add.15.total_ref
  119.4 1.3 put_terms.1
  120.8 12.4 %all-to-all-done.1.z_hbm = bf16[32,3,128,128]{3,2,1,0:T(8,128)(2,1)} async-done(((bf16[32,3,128,128]{3,2,1,0:T(8,128)(2,1)}), bf16[32,3,128,128]{3,2,1,0:T(8,128)(2,1)}, u32[]{:S(2)}, u32[]{:S(2)}) %all-to-all-start.1) | async-done | bytes 3145760 | tf_op jit(solution)/shard_map/all_to_all | solution.py:562
  133.1 5.0 %all-to-all-start.2 = ((bf16[32,136,128]{2,1,0:T(8,128)(2,1)}), bf16[32,136,128]{2,1,0:T(8,128)(2,1)S(1)}, u32[]{:S(2)}, u32[]{:S(2)}) async-start(bf16[32,136,128]{2,1,0:T(8,128)(2,1)} %put_terms.1), calls=%async_computation.2 | async-start | bytes 2228224 | tf_op jit(solution)/shard_map/all_to_all | solution.py:562
  138.1 3.0 %join_heads.1 = (bf16[1,128,4096]{2,1,0:T(8,128)(2,1)}, bf16[1,128,4096]{2,1,0:T(8,128)(2,1)}, bf16[1,128,4096]{2,1,0:T(8,128)(2,1)}) custom-call(bf16[32,3,128,128]{3,2,1,0:T(8,128)(2,1)} %all-to-all-done.1.z_hbm), custom_call_target="tpu_custom_call" | custom-call | tf_op jit(solution)/shard_map/join_heads/pallas_call | solution.py:526
  141.1 14.6 %all-to-all-done.2.z_ref = bf16[32,136,128]{2,1,0:T(8,128)(2,1)S(1)} async-done(((bf16[32,136,128]{2,1,0:T(8,128)(2,1)}), bf16[32,136,128]{2,1,0:T(8,128)(2,1)S(1)}, u32[]{:S(2)}, u32[]{:S(2)}) %all-to-all-start.2) | async-done | bytes 1114144 | tf_op jit(solution)/shard_map/all_to_all | solution.py:562
  155.8 1.7 %join_heads_terms.1 = (bf16[1,128,4096]{2,1,0:T(8,128)(2,1)}, f32[2,512]{1,0:T(2,128)}) custom-call(s32[1]{0:T(128)} %bitcast.place_ref, bf16[32,136,128]{2,1,0:T(8,128)(2,1)S(1)} %all-to-all-done.2.z_ref), custom_call_target="tpu_custom_call" | custom-call | tf_op jit(solution)/shard_map/join_heads_terms/pallas_call | solution.py:544
  (3 shorter events, 0.0 us)
Async XLA Ops:
  4.1 9.5 %copy-start.4 = (s32[1,32,3]{1,0,2:T(1,128)S(1)}, s32[1,32,3]{1,0,2:T(1,128)}, u32[]{:S(2)}) copy-start(s32[1,32,3]{1,0,2:T(1,128)} %param.15) | copy-start | bytes 1156
  4.1 9.6 %copy-start.3 = (f32[2,512]{1,0:T(2,128)S(1)}, f32[2,512]{1,0:T(2,128)}, u32[]{:S(2)}) copy-start(f32[2,512]{1,0:T(2,128)} %param.12) | copy-start | bytes 12292
  4.1 61.0 %copy-start.2 = (s32[1,2]{1,0:T(1,128)S(1)}, s32[1,2]{1,0:T(1,128)}, u32[]{:S(2)}) copy-start(s32[1,2]{1,0:T(1,128)} %global_ref.3) | copy-start | bytes 28
  4.1 61.0 %all-to-all-start = ((bf16[32,4,128,128]{3,2,1,0:T(8,128)(2,1)}), bf16[32,4,128,128]{3,2,1,0:T(8,128)(2,1)}, u32[]{:S(2)}, u32[]{:S(2)}) async-start(bf16[32,4,128,128]{3,2,1,0:T(8,128)(2,1)} %split_heads.1), calls=%async_computation | async-start | bytes 8388608 | tf_op jit(solution)/shard_map/all_to_all | solution.py:562
  13.7 72.4 %copy-start = (s32[1,32,3]{2,1,0:T(8,128)}, s32[1,32,3]{2,1,0:T(8,128)S(1)}, u32[]{:S(2)}) copy-start(s32[1,32,3]{2,1,0:T(8,128)S(1)} %copy.15.random_ref) | copy-start | bytes 1156
  38.0 48.2 %copy-start.1 = (f32[2,128]{1,0:T(2,128)}, f32[2,128]{1,0:T(2,128)S(1)}, u32[]{:S(2)}) copy-start(f32[2,128]{1,0:T(2,128)S(1)} %constant_dynamic-slice_fusion.gain_ref) | copy-start | bytes 3076
  86.1 47.0 %all-to-all-start.1 = ((bf16[32,3,128,128]{3,2,1,0:T(8,128)(2,1)}), bf16[32,3,128,128]{3,2,1,0:T(8,128)(2,1)}, u32[]{:S(2)}, u32[]{:S(2)}) async-start(bf16[32,3,128,128]{3,2,1,0:T(8,128)(2,1)} %get-tuple-element.17), calls=%async_computation.1 | async-start | bytes 6291456 | tf_op jit(solution)/shard_map/all_to_all | solution.py:562
  93.3 3.1 %collective-permute-start = (f32[2,128]{1,0:T(2,128)S(1)}, f32[2,128]{1,0:T(2,128)S(1)}, u32[]{:S(2)}, u32[]{:S(2)}) collective-permute-start(f32[2,128]{1,0:T(2,128)S(1)} %get-tuple-element.16), channel_id=1, source_target_pairs={{0,32},{32,0},{64,96},{96,64},{128,160},{160,128},{192,224},{224,1... | collective-permute-start | bytes 3080 | tf_op jit(solution)/shard_map/ppermute | solution.py:570
  96.4 4.3 %collective-permute-start.1 = (f32[2,128]{1,0:T(2,128)S(1)}, f32[2,128]{1,0:T(2,128)S(1)}, u32[]{:S(2)}, u32[]{:S(2)}) collective-permute-start(f32[2,128]{1,0:T(2,128)S(1)} %add.13), channel_id=1, source_target_pairs={{0,64},{32,96},{64,0},{96,32},{128,192},{160,224},{192,128},{224,1... | collective-permute-start | bytes 3080 | tf_op jit(solution)/shard_map/ppermute | solution.py:570
  100.8 18.1 %collective-permute-start.2 = (f32[2,128]{1,0:T(2,128)S(1)}, f32[2,128]{1,0:T(2,128)S(1)}, u32[]{:S(2)}, u32[]{:S(2)}) collective-permute-start(f32[2,128]{1,0:T(2,128)S(1)} %add.14), channel_id=1, source_target_pairs={{0,128},{32,160},{64,192},{96,224},{128,0},{160,32},{192,64},{224,... | collective-permute-start | bytes 3080 | tf_op jit(solution)/shard_map/ppermute | solution.py:570
  133.1 22.6 %all-to-all-start.2 = ((bf16[32,136,128]{2,1,0:T(8,128)(2,1)}), bf16[32,136,128]{2,1,0:T(8,128)(2,1)S(1)}, u32[]{:S(2)}, u32[]{:S(2)}) async-start(bf16[32,136,128]{2,1,0:T(8,128)(2,1)} %put_terms.1), calls=%async_computation.2 | async-start | bytes 2228224 | tf_op jit(solution)/shard_map/all_to_all | solution.py:562
